TPU v7x, 32 devices: a whole 2x2x4 slice. The times are simulated.
32 devices in a mesh: dp: 4 (over y, core), fsdp: 8 (over z, x).
Axes of the slice: x: 2, y: 2, z: 4, core: 2. Of those that a mesh axis runs over, the one named last changes fastest.
Arguments:
- tokens: bfloat16 [32768, 576], P(('dp', 'fsdp')), may hold values from -6 to 6
- segments: int32 [32, 1024], P(('dp', 'fsdp')), may hold values from 0 to 2, as said below
- positions: int32 [32, 1024], P(('dp', 'fsdp')), may hold values from 0 to 2302, as said below
- attn_gain: bfloat16 [576], P('fsdp'), may hold values from 0.25 to 1.75
- mlp_gain: bfloat16 [576], P('fsdp'), may hold values from 0.25 to 1.75
- w_query: bfloat16 [576, 576], P('fsdp', 'dp'), may hold values from -0.375 to 0.375
- w_key: bfloat16 [576, 192], P('fsdp', 'dp'), may hold values from -0.375 to 0.375
- w_value: bfloat16 [576, 192], P('fsdp', 'dp'), may hold values from -0.25 to 0.25
- w_output: bfloat16 [576, 576], P('dp', 'fsdp'), may hold values from -1 to 1
- w_gate: bfloat16 [576, 1536], P('fsdp', 'dp'), may hold values from -0.25 to 0.25
- w_up: bfloat16 [576, 1536], P('fsdp', 'dp'), may hold values from -0.25 to 0.25
- w_down: bfloat16 [1536, 576], P('dp', 'fsdp'), may hold values from -0.21875 to 0.21875
- cotangent: bfloat16 [32768, 576], P(('dp', 'fsdp')), may hold values from -6 to 6
Outputs:
- output: bfloat16 [32768, 576], P(('dp', 'fsdp'))
- grad_tokens: float32 [32768, 576], P(('dp', 'fsdp'))
- grad_attn_gain: float32 [576], P('fsdp')
- grad_mlp_gain: float32 [576], P('fsdp')
- grad_query: float32 [576, 576], P('fsdp', 'dp')
- grad_key: float32 [576, 192], P('fsdp', 'dp')
- grad_value: float32 [576, 192], P('fsdp', 'dp')
- grad_output: float32 [576, 576], P('dp', 'fsdp')
- grad_gate: float32 [576, 1536], P('fsdp', 'dp')
- grad_up: float32 [576, 1536], P('fsdp', 'dp')
- grad_down: float32 [1536, 576], P('dp', 'fsdp')
Inputs may be any that keep to these rules, and one draw needn't show every extreme that they name: `segments`: in each sequence the document numbers are 0, then 1, then 2, each a run of 128 tokens or more. `positions`: counts up by one along a document; documents 1 and 2 of a sequence begin at 0, document 0 continues a document begun at most 2047 tokens before the sequence and ends within its first 256 tokens.
All inputs are finite; a program needn't handle non-finite values.
Results may differ from a plain program's by a relative error of at most 0.015.
The roundings to bfloat16 on the way count: a program that leaves them out, or rounds other values in their place, can miss the bound.
Values may be sent and summed in bfloat16 or wider, within the bound.
A program may use at most 192 MiB of HBM per device.

v0:
```python
import jax
import jax.numpy as jnp
from jax import lax
from jax.sharding import PartitionSpec as P

Q_HEADS = 9
KV_HEADS = 3
HEAD_DIM = 64
LEN = 1024
QBLOCK = 512
QW = 576
KVW = 192


EPS = 1e-05
ROPE_BASE = 100000.0
MASKED = -1e30


def tables(position):
    half_dim = HEAD_DIM // 2
    frequency = ROPE_BASE ** (-(2.0 * jnp.arange(half_dim, dtype=jnp.float32)) / HEAD_DIM)
    angles = position.astype(jnp.float32)[:, None] * frequency[None, :]
    angles = jnp.concatenate([angles, angles], axis=1)
    return (jnp.cos(angles), jnp.sin(angles))


def rotate(values, cosine, sine_table):
    half_dim = HEAD_DIM // 2
    turned = jnp.concatenate([-values[..., half_dim:], values[..., :half_dim]], axis=-1)
    return values * cosine[:, None, :] + turned * sine_table[:, None, :]


def rotate_back(grads, cosine, sine_table):
    half_dim = HEAD_DIM // 2
    scaled = grads * sine_table[:, None, :]
    return grads * cosine[:, None, :] + jnp.concatenate(
        [scaled[..., half_dim:], -scaled[..., :half_dim]], axis=-1
    )


def norm_rows(values):
    inverse = lax.rsqrt(jnp.mean(values * values, axis=-1, keepdims=True) + EPS)
    return (values * inverse, inverse)


def norm_back(grad_scaled, scaled, inverse):
    return inverse * (grad_scaled - scaled * jnp.mean(grad_scaled * scaled, axis=-1, keepdims=True))


def block_scores(queries, keys, segment, block_index, kv_head):
    group_size = Q_HEADS // KV_HEADS
    first_row = block_index * QBLOCK
    row_index = first_row + jnp.arange(QBLOCK, dtype=jnp.int32)
    col_index = jnp.arange(LEN, dtype=jnp.int32)
    seg_block = segment[first_row : first_row + QBLOCK]
    allowed = (col_index[None, :] <= row_index[:, None]) & (segment[None, :] == seg_block[:, None])
    width = group_size * HEAD_DIM
    query_block = queries[
        first_row : first_row + QBLOCK, kv_head * width : (kv_head + 1) * width
    ].reshape(QBLOCK, group_size, HEAD_DIM)
    key_head = keys[:, kv_head * HEAD_DIM : (kv_head + 1) * HEAD_DIM]
    scores = jnp.einsum(
        "qgd,td->gqt", query_block, key_head, preferred_element_type=jnp.float32
    ) * HEAD_DIM ** (-0.5)
    return (query_block, key_head, jnp.where(allowed[None], scores, MASKED))


def attend_forward(sequence):
    queries, keys, values, segment = sequence
    group_size = Q_HEADS // KV_HEADS
    block_rows, top_list, total_list = ([], [], [])
    for block_index in range(LEN // QBLOCK):
        head_rows, head_tops, head_totals = ([], [], [])
        for kv_head in range(KV_HEADS):
            query_block, key_head, scores = block_scores(
                queries, keys, segment, block_index, kv_head
            )
            top_value = jnp.max(scores, axis=-1, keepdims=True)
            expo = jnp.exp(scores - top_value)
            total = jnp.sum(expo, axis=-1, keepdims=True)
            probability = (expo / total).astype(jnp.bfloat16)
            value_head = values[:, kv_head * HEAD_DIM : (kv_head + 1) * HEAD_DIM]
            attended = jnp.einsum(
                "gqt,td->qgd", probability, value_head, preferred_element_type=jnp.float32
            )
            head_rows.append(attended.reshape(QBLOCK, group_size * HEAD_DIM))
            head_tops.append(top_value)
            head_totals.append(total)
        block_rows.append(jnp.concatenate(head_rows, axis=1))
        top_list.append(jnp.stack(head_tops))
        total_list.append(jnp.stack(head_totals))
    mixture = jnp.concatenate(block_rows, axis=0).astype(jnp.bfloat16)
    return (mixture, jnp.stack(top_list), jnp.stack(total_list))


def attend_backward(sequence):
    queries, keys, values, segment, tops, totals, grad_mixture = sequence
    group_size = Q_HEADS // KV_HEADS
    scale = HEAD_DIM ** (-0.5)
    width = group_size * HEAD_DIM
    grad_key_heads = [jnp.zeros((LEN, HEAD_DIM), jnp.float32) for kv_head in range(KV_HEADS)]
    grad_value_heads = [jnp.zeros((LEN, HEAD_DIM), jnp.float32) for kv_head in range(KV_HEADS)]
    block_rows = []
    for block_index in range(LEN // QBLOCK):
        first_row = block_index * QBLOCK
        head_rows = []
        for kv_head in range(KV_HEADS):
            query_block, key_head, scores = block_scores(
                queries, keys, segment, block_index, kv_head
            )
            expo = jnp.exp(scores - tops[block_index, kv_head])
            prob_full = expo / totals[block_index, kv_head]
            probability = prob_full.astype(jnp.bfloat16)
            value_head = values[:, kv_head * HEAD_DIM : (kv_head + 1) * HEAD_DIM]
            grad_block = grad_mixture[
                first_row : first_row + QBLOCK, kv_head * width : (kv_head + 1) * width
            ].reshape(QBLOCK, group_size, HEAD_DIM)
            grad_probs = jnp.einsum(
                "qgd,td->gqt", grad_block, value_head, preferred_element_type=jnp.float32
            )
            grad_value_heads[kv_head] = grad_value_heads[kv_head] + jnp.einsum(
                "gqt,qgd->td", probability, grad_block, preferred_element_type=jnp.float32
            )
            delta = jnp.sum(prob_full * grad_probs, axis=-1, keepdims=True)
            grad_scores = (prob_full * (grad_probs - delta)).astype(jnp.bfloat16)
            grad_query_block = (
                jnp.einsum("gqt,td->qgd", grad_scores, key_head, preferred_element_type=jnp.float32)
                * scale
            )
            grad_key_heads[kv_head] = (
                grad_key_heads[kv_head]
                + jnp.einsum(
                    "gqt,qgd->td", grad_scores, query_block, preferred_element_type=jnp.float32
                )
                * scale
            )
            head_rows.append(grad_query_block.reshape(QBLOCK, width))
        block_rows.append(jnp.concatenate(head_rows, axis=1))
    grad_queries = jnp.concatenate(block_rows, axis=0)
    return (
        grad_queries,
        jnp.concatenate(grad_key_heads, axis=1),
        jnp.concatenate(grad_value_heads, axis=1),
    )


def on_device(
    tokens,
    segments,
    positions,
    attn_gain,
    mlp_gain,
    w_query,
    w_key,
    w_value,
    w_output,
    w_gate,
    w_up,
    w_down,
    cotangent,
):
    columns = (
        lax.all_gather(w_query, "dp", axis=1, tiled=True),
        lax.all_gather(w_key, "dp", axis=1, tiled=True),
        lax.all_gather(w_value, "dp", axis=1, tiled=True),
        lax.all_gather(w_output, "dp", axis=0, tiled=True),
        lax.all_gather(w_gate, "dp", axis=1, tiled=True),
        lax.all_gather(w_up, "dp", axis=1, tiled=True),
        lax.all_gather(w_down, "dp", axis=0, tiled=True),
    )
    weights = (
        lax.all_gather(attn_gain, "fsdp", axis=0, tiled=True),
        lax.all_gather(mlp_gain, "fsdp", axis=0, tiled=True),
        lax.all_gather(columns[0], "fsdp", axis=0, tiled=True),
        lax.all_gather(columns[1], "fsdp", axis=0, tiled=True),
        lax.all_gather(columns[2], "fsdp", axis=0, tiled=True),
        lax.all_gather(columns[3], "fsdp", axis=1, tiled=True),
        lax.all_gather(columns[4], "fsdp", axis=0, tiled=True),
        lax.all_gather(columns[5], "fsdp", axis=0, tiled=True),
        lax.all_gather(columns[6], "fsdp", axis=1, tiled=True),
    )
    row_count = tokens.shape[0]
    seq_count = segments.shape[0]
    gain_attn = weights[0].astype(jnp.float32)
    gain_mlp = weights[1].astype(jnp.float32)
    inputs = tokens.astype(jnp.float32)
    cosine, sine_table = tables(positions.reshape(row_count))
    scaled_attn, inverse_attn = norm_rows(inputs)
    normed_attn = (scaled_attn * gain_attn).astype(jnp.bfloat16)
    query_raw = jnp.dot(normed_attn, weights[2], preferred_element_type=jnp.float32)
    key_raw = jnp.dot(normed_attn, weights[3], preferred_element_type=jnp.float32)
    value_raw = jnp.dot(normed_attn, weights[4], preferred_element_type=jnp.float32)
    queries = (
        rotate(query_raw.reshape(row_count, Q_HEADS, HEAD_DIM), cosine, sine_table)
        .reshape(row_count, QW)
        .astype(jnp.bfloat16)
    )
    keys = (
        rotate(key_raw.reshape(row_count, KV_HEADS, HEAD_DIM), cosine, sine_table)
        .reshape(row_count, KVW)
        .astype(jnp.bfloat16)
    )
    values = value_raw.astype(jnp.bfloat16)
    seq_queries = queries.reshape(seq_count, LEN, QW)
    seq_keys = keys.reshape(seq_count, LEN, KVW)
    seq_values = values.reshape(seq_count, LEN, KVW)
    mixture, tops, totals = lax.map(attend_forward, (seq_queries, seq_keys, seq_values, segments))
    mixture = mixture.reshape(row_count, QW)
    resid = inputs + jnp.dot(mixture, weights[5], preferred_element_type=jnp.float32)
    scaled_mlp, inverse_mlp = norm_rows(resid)
    normed_mlp = (scaled_mlp * gain_mlp).astype(jnp.bfloat16)
    gate_pre = jnp.dot(normed_mlp, weights[6], preferred_element_type=jnp.float32)
    up_pre = jnp.dot(normed_mlp, weights[7], preferred_element_type=jnp.float32)
    hidden = (jax.nn.silu(gate_pre) * up_pre).astype(jnp.bfloat16)
    output = (resid + jnp.dot(hidden, weights[8], preferred_element_type=jnp.float32)).astype(
        jnp.bfloat16
    )
    again = (
        lax.all_gather(w_query, "dp", axis=1, tiled=True),
        lax.all_gather(w_key, "dp", axis=1, tiled=True),
        lax.all_gather(w_value, "dp", axis=1, tiled=True),
        lax.all_gather(w_output, "dp", axis=0, tiled=True),
        lax.all_gather(w_gate, "dp", axis=1, tiled=True),
        lax.all_gather(w_up, "dp", axis=1, tiled=True),
        lax.all_gather(w_down, "dp", axis=0, tiled=True),
    )
    back_weights = (
        lax.all_gather(attn_gain, "fsdp", axis=0, tiled=True),
        lax.all_gather(mlp_gain, "fsdp", axis=0, tiled=True),
        lax.all_gather(again[0], "fsdp", axis=0, tiled=True),
        lax.all_gather(again[1], "fsdp", axis=0, tiled=True),
        lax.all_gather(again[2], "fsdp", axis=0, tiled=True),
        lax.all_gather(again[3], "fsdp", axis=1, tiled=True),
        lax.all_gather(again[4], "fsdp", axis=0, tiled=True),
        lax.all_gather(again[5], "fsdp", axis=0, tiled=True),
        lax.all_gather(again[6], "fsdp", axis=1, tiled=True),
    )
    grad_down = jnp.einsum("rf,rd->fd", hidden, cotangent, preferred_element_type=jnp.float32)
    grad_hidden = jnp.einsum(
        "rd,fd->rf", cotangent, back_weights[8], preferred_element_type=jnp.float32
    )
    sigmoid = jax.nn.sigmoid(gate_pre)
    grad_gate_pre = (grad_hidden * up_pre * sigmoid * (1.0 + gate_pre * (1.0 - sigmoid))).astype(
        jnp.bfloat16
    )
    grad_up_pre = (grad_hidden * (gate_pre * sigmoid)).astype(jnp.bfloat16)
    grad_gate = jnp.einsum(
        "rd,rf->df", normed_mlp, grad_gate_pre, preferred_element_type=jnp.float32
    )
    grad_up = jnp.einsum("rd,rf->df", normed_mlp, grad_up_pre, preferred_element_type=jnp.float32)
    grad_normed_mlp = jnp.einsum(
        "rf,df->rd", grad_gate_pre, back_weights[6], preferred_element_type=jnp.float32
    )
    grad_normed_mlp = grad_normed_mlp + jnp.einsum(
        "rf,df->rd", grad_up_pre, back_weights[7], preferred_element_type=jnp.float32
    )
    grad_mlp_gain = jnp.sum(grad_normed_mlp * scaled_mlp, axis=0)
    grad_resid = cotangent.astype(jnp.float32) + norm_back(
        grad_normed_mlp * back_weights[1].astype(jnp.float32), scaled_mlp, inverse_mlp
    )
    grad_branch = grad_resid.astype(jnp.bfloat16)
    grad_output = jnp.einsum("rq,rd->qd", mixture, grad_branch, preferred_element_type=jnp.float32)
    grad_mixture = jnp.einsum(
        "rd,qd->rq", grad_branch, back_weights[5], preferred_element_type=jnp.float32
    ).astype(jnp.bfloat16)
    grad_queries, grad_keys, grad_values = lax.map(
        attend_backward,
        (
            seq_queries,
            seq_keys,
            seq_values,
            segments,
            tops,
            totals,
            grad_mixture.reshape(seq_count, LEN, QW),
        ),
    )
    grad_query_raw = (
        rotate_back(grad_queries.reshape(row_count, Q_HEADS, HEAD_DIM), cosine, sine_table)
        .reshape(row_count, QW)
        .astype(jnp.bfloat16)
    )
    grad_key_raw = (
        rotate_back(grad_keys.reshape(row_count, KV_HEADS, HEAD_DIM), cosine, sine_table)
        .reshape(row_count, KVW)
        .astype(jnp.bfloat16)
    )
    grad_value_raw = grad_values.reshape(row_count, KVW).astype(jnp.bfloat16)
    grad_query = jnp.einsum(
        "rd,rq->dq", normed_attn, grad_query_raw, preferred_element_type=jnp.float32
    )
    grad_key = jnp.einsum(
        "rd,rq->dq", normed_attn, grad_key_raw, preferred_element_type=jnp.float32
    )
    grad_value = jnp.einsum(
        "rd,rq->dq", normed_attn, grad_value_raw, preferred_element_type=jnp.float32
    )
    grad_normed_attn = jnp.einsum(
        "rq,dq->rd", grad_query_raw, back_weights[2], preferred_element_type=jnp.float32
    )
    grad_normed_attn = grad_normed_attn + jnp.einsum(
        "rq,dq->rd", grad_key_raw, back_weights[3], preferred_element_type=jnp.float32
    )
    grad_normed_attn = grad_normed_attn + jnp.einsum(
        "rq,dq->rd", grad_value_raw, back_weights[4], preferred_element_type=jnp.float32
    )
    grad_attn_gain = jnp.sum(grad_normed_attn * scaled_attn, axis=0)
    grad_tokens = grad_resid + norm_back(
        grad_normed_attn * back_weights[0].astype(jnp.float32), scaled_attn, inverse_attn
    )
    replicas = lax.axis_size("dp")
    first_sums = (
        lax.psum_scatter(grad_attn_gain, "fsdp", scatter_dimension=0, tiled=True),
        lax.psum_scatter(grad_mlp_gain, "fsdp", scatter_dimension=0, tiled=True),
        lax.psum_scatter(grad_query, "fsdp", scatter_dimension=0, tiled=True),
        lax.psum_scatter(grad_key, "fsdp", scatter_dimension=0, tiled=True),
        lax.psum_scatter(grad_value, "fsdp", scatter_dimension=0, tiled=True),
        lax.psum_scatter(grad_output, "fsdp", scatter_dimension=1, tiled=True),
        lax.psum_scatter(grad_gate, "fsdp", scatter_dimension=0, tiled=True),
        lax.psum_scatter(grad_up, "fsdp", scatter_dimension=0, tiled=True),
        lax.psum_scatter(grad_down, "fsdp", scatter_dimension=1, tiled=True),
    )
    spread_attn = jnp.broadcast_to(first_sums[0][:, None], (first_sums[0].shape[0], replicas))
    spread_mlp = jnp.broadcast_to(first_sums[1][:, None], (first_sums[1].shape[0], replicas))
    final_sums = (
        lax.psum_scatter(spread_attn, "dp", scatter_dimension=1, tiled=True),
        lax.psum_scatter(spread_mlp, "dp", scatter_dimension=1, tiled=True),
        lax.psum_scatter(first_sums[2], "dp", scatter_dimension=1, tiled=True),
        lax.psum_scatter(first_sums[3], "dp", scatter_dimension=1, tiled=True),
        lax.psum_scatter(first_sums[4], "dp", scatter_dimension=1, tiled=True),
        lax.psum_scatter(first_sums[5], "dp", scatter_dimension=0, tiled=True),
        lax.psum_scatter(first_sums[6], "dp", scatter_dimension=1, tiled=True),
        lax.psum_scatter(first_sums[7], "dp", scatter_dimension=1, tiled=True),
        lax.psum_scatter(first_sums[8], "dp", scatter_dimension=0, tiled=True),
    )
    return (
        output,
        grad_tokens,
        final_sums[0][:, 0],
        final_sums[1][:, 0],
        final_sums[2],
        final_sums[3],
        final_sums[4],
        final_sums[5],
        final_sums[6],
        final_sums[7],
        final_sums[8],
    )


def solution(mesh):
    in_specs = (
        P(("dp", "fsdp"), None),
        P(("dp", "fsdp"), None),
        P(("dp", "fsdp"), None),
        P("fsdp"),
        P("fsdp"),
        P("fsdp", "dp"),
        P("fsdp", "dp"),
        P("fsdp", "dp"),
        P("dp", "fsdp"),
        P("fsdp", "dp"),
        P("fsdp", "dp"),
        P("dp", "fsdp"),
        P(("dp", "fsdp"), None),
    )
    out_specs = (
        P(("dp", "fsdp"), None),
        P(("dp", "fsdp"), None),
        P("fsdp"),
        P("fsdp"),
        P("fsdp", "dp"),
        P("fsdp", "dp"),
        P("fsdp", "dp"),
        P("dp", "fsdp"),
        P("fsdp", "dp"),
        P("fsdp", "dp"),
        P("dp", "fsdp"),
    )
    return jax.shard_map(
        on_device, mesh=mesh, in_specs=in_specs, out_specs=out_specs, check_vma=False
    )
```

profile of v0, /device:TPU:0, one launch (start us, length us, event | category | flops | bytes accessed | tf_op | source)
XLA Modules:
  0.0 1057.9 jit_solution(8182386799139232745)
XLA Ops:
  7.3 8.9 all_gather.74
  16.2 6.6 all_gather.76
  22.9 7.4 all_gather.78
  30.4 5.7 all_gather.71
  37.1 5.5 all_gather.69
  42.7 33.7 %all_gather.70 = bf16[576,576]{1,0:T(8,128)(2,1)S(1)} all-gather(bf16[72,576]{1,0:T(8,128)(2,1)S(1)} %copy.85), channel_id=1, replica_groups=mesh['dp'=4,'fsdp'=8] {'fsdp'}, dimensions={0}, use_global_device_ids=true | all-gather | bytes 746496 | tf_op jit(solution)/shard_map/all_gather | solution.py:175
  78.2 21.5 %all-reduce.10 = (bf16[576]{0:T(1024)(128)(2,1)S(1)}, bf16[576]{0:T(1024)(128)(2,1)S(1)}) all-reduce(bf16[576]{0:T(1024)(128)(2,1)S(1)} %dynamic-update-slice, bf16[576]{0:T(1024)(128)(2,1)S(1)} %dynamic-update-slice.1), channel_id=1, replica_groups=mesh['dp'=4,'fsdp'=8] {'fsdp'}, use_global_device_ids=true, to_apply=%add | all-reduce | flops 1152 | bytes 4608
  104.0 5.2 all_gather.67
  109.3 31.3 %all_gather.68 = bf16[576,192]{1,0:T(8,128)(2,1)S(1)} all-gather(bf16[72,192]{1,0:T(8,128)(2,1)S(1)} %copy.83), channel_id=1, replica_groups=mesh['dp'=4,'fsdp'=8] {'fsdp'}, dimensions={0}, use_global_device_ids=true | all-gather | bytes 248832 | tf_op jit(solution)/shard_map/all_gather | solution.py:176
  142.1 3.7 fusion.134
  145.8 3.6 fusion.135
  149.4 5.2 all_gather.65
  154.7 31.7 %all_gather.66 = bf16[576,192]{1,0:T(8,128)(2,1)S(1)} all-gather(bf16[72,192]{1,0:T(8,128)(2,1)S(1)} %copy.82), channel_id=1, replica_groups=mesh['dp'=4,'fsdp'=8] {'fsdp'}, dimensions={0}, use_global_device_ids=true | all-gather | bytes 248832 | tf_op jit(solution)/shard_map/all_gather | solution.py:177
  192.4 5.1 fusion.19
  197.7 3.4 fusion.22
  201.1 9.6 fusion.20
  210.8 2.0 fusion.66
  214.9 2.0 fusion.68
  217.0 2.0 fusion.69
  219.1 2.0 fusion.70
  221.2 2.0 fusion.71
  223.3 32.0 %all_gather.72 = bf16[576,576]{0,1:T(8,128)(2,1)S(1)} all-gather(bf16[576,72]{0,1:T(8,128)(2,1)S(1)} %copy.92), channel_id=1, replica_groups=mesh['dp'=4,'fsdp'=8] {'fsdp'}, dimensions={1}, use_global_device_ids=true | all-gather | bytes 746496 | tf_op jit(solution)/shard_map/all_gather | solution.py:178
  260.4 5.9 fusion.168
  266.3 7.2 fusion.169
  273.6 10.5 multiply_convert_fusion
  286.9 3.0 multiply_reduce_fusion
  292.4 3.8 fusion.129
  296.2 3.6 fusion.133
  299.9 2.7 fusion.84
  302.7 2.7 fusion.78
  305.5 2.7 fusion.72
  308.2 11.6 %fusion.15 = (f32[3,512]{1,0:T(4,128)S(1)}, f32[3,512]{1,0:T(4,128)S(1)}, f32[3,512]{1,0:T(4,128)S(1)}, f32[1024,512,3]{1,0,2:T(8,128)}) fusion(f32[3,512]{1,0:T(4,128)S(1)} %copy-done.77, f32[3,512]{1,0:T(4,128)S(1)} %copy-done.80, f32[1024,512,3]{1,0,2:T(8,128)} %copy-done.10, pred[512,1024]{0,1:T(8,128)(4,1)S(1)} %copy-done.17, ...), kind=kOutput, calls=%fused_computation.27 | convolution fusion | flops 229633536 | bytes 38668288 | tf_op jit(solution)/shard_map/while/body/eval_jaxpr/qgd,td->gqt/dot_general | solution.py:119
  319.7 12.3 %fusion.17 = (bf16[3,512,1024]{1,2,0:T(8,128)(2,1)S(1)}, bf16[3,512,1024]{1,2,0:T(8,128)(2,1)S(1)}, bf16[3,512,1024]{1,2,0:T(8,128)(2,1)S(1)}) fusion(f32[1024,512,3]{1,0,2:T(8,128)} %get-tuple-element.186, f32[3,512]{1,0:T(4,128)S(1)} %get-tuple-element.105, f32[3,512]{1,0:T(4,128)S(1)} %copy-done.77, f32[3,512]{1,0:T(4,128)S(1)} %copy-done.80, ...), kind=kLoop, calls=%fused_computation.29 | loop fusion | flops 33030144 | bytes 47765504 | tf_op jit(solution)/shard_map/while/body/eval_jaxpr/convert_element_type | solution.py:126
  338.3 3.6 fusion.128
  342.0 3.6 fusion.132
  345.7 12.8 %fusion.6 = (f32[3,512]{1,0:T(4,128)S(1)}, f32[3,512]{1,0:T(4,128)S(1)}, f32[3,512]{1,0:T(4,128)S(1)}, f32[1024,512,3]{1,0,2:T(8,128)}) fusion(f32[3,512]{1,0:T(4,128)S(1)} %get-tuple-element.169, f32[3,512]{1,0:T(4,128)S(1)} %copy-done.67, f32[1024,512,3]{1,0,2:T(8,128)} %copy-done.9, pred[512,1024]{0,1:T(8,128)(4,1)S(1)} %copy-done.14, ...), kind=kOutput, calls=%fused_computation.12 | convolution fusion | flops 229633536 | bytes 38668288 | tf_op jit(solution)/shard_map/while/body/eval_jaxpr/qgd,td->gqt/dot_general | solution.py:119
  358.5 12.5 %fusion.8 = (bf16[3,512,1024]{1,2,0:T(8,128)(2,1)S(1)}, bf16[3,512,1024]{1,2,0:T(8,128)(2,1)S(1)}, bf16[3,512,1024]{1,2,0:T(8,128)(2,1)S(1)}) fusion(f32[1024,512,3]{1,0,2:T(8,128)} %get-tuple-element.185, f32[3,512]{1,0:T(4,128)S(1)} %get-tuple-element.108, f32[3,512]{1,0:T(4,128)S(1)} %get-tuple-element.169, f32[3,512]{1,0:T(4,128)S(1)} %copy-done.67, ...), kind=kLoop, calls=%fused_computation.14 | loop fusion | flops 33030144 | bytes 47765504 | tf_op jit(solution)/shard_map/while/body/eval_jaxpr/convert_element_type | solution.py:126
  380.4 2.3 fusion.155
  387.2 5.7 fusion.111
  393.0 2.6 fusion.108
  396.0 4.9 fusion.105
  402.6 4.3 fusion.118
  406.9 5.7 fusion.171
  412.7 5.7 fusion.172
  419.7 5.7 fusion.175
  425.4 18.7 %reduce-scatter.51.cloned.1.call-done = f32[72,576]{1,0:T(8,128)} async-done(((f32[576,576]{1,0:T(8,128)}), f32[72,576]{1,0:T(8,128)}) %reduce-scatter.51.cloned.1.call-update) | async-done | bytes 165904
  446.0 63.1 %reduce-scatter.27.cloned.1.call-done = f32[72,192]{1,0:T(8,128)} async-done(((f32[576,192]{1,0:T(8,128)}), f32[72,192]{1,0:T(8,128)}) %reduce-scatter.27.cloned.1.call-update) | async-done | bytes 55312 | tf_op jit(solution)/shard_map/reduce_scatter | solution.py:317
  510.8 63.3 %reduce-scatter.29.cloned.1.call-done = f32[72,192]{1,0:T(8,128)} async-done(((f32[576,192]{1,0:T(8,128)}), f32[72,192]{1,0:T(8,128)}) %reduce-scatter.29.cloned.1.call-update) | async-done | bytes 55312 | tf_op jit(solution)/shard_map/reduce_scatter | solution.py:318
  575.7 64.8 %reduce-scatter.53.cloned.1.call-done = f32[576,72]{0,1:T(8,128)} async-done(((f32[576,576]{0,1:T(8,128)}), f32[576,72]{0,1:T(8,128)}) %reduce-scatter.53.cloned.1.call-update) | async-done | bytes 165904
  642.4 80.3 %reduce-scatter.31.cloned.1.call-done = f32[72,1536]{1,0:T(8,128)} async-done(((f32[576,1536]{1,0:T(8,128)}), f32[72,1536]{1,0:T(8,128)}) %reduce-scatter.31.cloned.1.call-update) | async-done | bytes 442384 | tf_op jit(solution)/shard_map/reduce_scatter | solution.py:320
  724.1 3.7 fusion.173
  727.7 77.7 %reduce-scatter.35.cloned.1.call-done = f32[72,1536]{1,0:T(8,128)} async-done(((f32[576,1536]{1,0:T(8,128)}), f32[72,1536]{1,0:T(8,128)}) %reduce-scatter.35.cloned.1.call-update) | async-done | bytes 442384 | tf_op jit(solution)/shard_map/reduce_scatter | solution.py:321
  807.2 2.4 fusion.58
  809.5 78.5 %reduce-scatter.39.cloned.1.call-done = f32[1536,72]{0,1:T(8,128)} async-done(((f32[1536,576]{0,1:T(8,128)}), f32[1536,72]{0,1:T(8,128)}) %reduce-scatter.39.cloned.1.call-update) | async-done | bytes 442384 | tf_op jit(solution)/shard_map/reduce_scatter | solution.py:322
  888.0 4.5 fusion.57
  892.5 20.4 %all-reduce.8 = (f32[576]{0:T(1024)S(1)}, f32[576]{0:T(1024)S(1)}) all-reduce(f32[576]{0:T(1024)S(1)} %get-tuple-element.103, f32[576]{0:T(1024)S(1)} %copy-done.85), channel_id=2, replica_groups=mesh['dp'=4,'fsdp'=8] {'fsdp'}, use_global_device_ids=true, to_apply=%region_23.24.clone | all-reduce | flops 1152 | bytes 9216
  913.1 5.6 all-reduce.9
  921.0 5.7 add_convert_fusion
  928.3 4.6 reduce-scatter.45.cloned.1.call-done
  932.9 22.6 %reduce-scatter.47.cloned.1.call-done = f32[48,72]{1,0:T(8,128)} async-done(((f32[192,72]{1,0:T(8,128)}), f32[48,72]{1,0:T(8,128)}) %reduce-scatter.47.cloned.1.call-update) | async-done | bytes 13840
  955.5 23.2 %reduce-scatter.49.cloned.1.call-done = f32[144,72]{1,0:T(8,128)} async-done(((f32[576,72]{1,0:T(8,128)}), f32[144,72]{1,0:T(8,128)}) %reduce-scatter.49.cloned.1.call-update) | async-done | bytes 41488
  978.7 24.1 %reduce-scatter.33.cloned.1.call-done = f32[72,384]{1,0:T(8,128)} async-done(((f32[72,1536]{1,0:T(8,128)}), f32[72,384]{1,0:T(8,128)}) %reduce-scatter.33.cloned.1.call-update) | async-done | bytes 110608 | tf_op jit(solution)/shard_map/reduce_scatter | solution.py:333
  1002.8 24.1 %reduce-scatter.37.cloned.1.call-done = f32[72,384]{1,0:T(8,128)} async-done(((f32[72,1536]{1,0:T(8,128)}), f32[72,384]{1,0:T(8,128)}) %reduce-scatter.37.cloned.1.call-update) | async-done | bytes 110608 | tf_op jit(solution)/shard_map/reduce_scatter | solution.py:334
  1026.9 24.1 %reduce-scatter.41.cloned.1.call-done = f32[384,72]{0,1:T(8,128)} async-done(((f32[1536,72]{0,1:T(8,128)}), f32[384,72]{0,1:T(8,128)}) %reduce-scatter.41.cloned.1.call-update) | async-done | bytes 110608 | tf_op jit(solution)/shard_map/reduce_scatter | solution.py:335
  (388 shorter events, 63.5 us)
Async XLA Ops:
  7.2 69.2 %copy-start.86 = (u32[32]{0:T(128)S(1)}, u32[32]{0:T(128)}, u32[]{:S(2)}) copy-start(u32[32]{0:T(128)} %constant.87) | copy-start | bytes 388
  7.2 70.5 %copy-start.90 = (bf16[72]{0:T(256)(128)(2,1)S(1)}, bf16[72]{0:T(256)(128)(2,1)}, u32[]{:S(2)}) copy-start(bf16[72]{0:T(256)(128)(2,1)} %param.16) | copy-start | bytes 436
  7.2 70.7 %copy-start.91 = (bf16[72]{0:T(256)(128)(2,1)S(1)}, bf16[72]{0:T(256)(128)(2,1)}, u32[]{:S(2)}) copy-start(bf16[72]{0:T(256)(128)(2,1)} %param.17) | copy-start | bytes 436
  7.2 92.5 %copy-start.1 = (bf16[1024,576]{0,1:T(8,128)(2,1)S(1)}, bf16[1024,576]{0,1:T(8,128)(2,1)}, u32[]{:S(2)}) copy-start(bf16[1024,576]{0,1:T(8,128)(2,1)} %param.13) | copy-start | bytes 3538948
  7.2 252.2 %all-gather.4.cloned.1.call-start = ((), (), s32[]{:S(2)}) async-start(), calls=%async_computation.14 | async-start | bytes 1990656 | tf_op jit(solution)/shard_map/all_gather | solution.py:179
  16.1 250.2 %all-gather.6.cloned.1.call-start = ((), (), s32[]{:S(2)}) async-start(), calls=%async_computation.15 | async-start | bytes 1990656 | tf_op jit(solution)/shard_map/all_gather | solution.py:180
  22.8 250.7 %all-gather.8.cloned.1.call-start = ((), (), s32[]{:S(2)}) async-start(), calls=%async_computation.16 | async-start | bytes 1990656 | tf_op jit(solution)/shard_map/all_gather | solution.py:181
  30.3 413.9 %reduce-scatter.51.cloned.1.call-start = ((), (), s32[]{:S(2)}) async-start(), calls=%async_computation.29 | async-start | bytes 1658880
  76.3 24.8 %copy-start.51 = (bf16[576,576]{1,0:T(8,128)(2,1)}, bf16[576,576]{1,0:T(8,128)(2,1)S(1)}, u32[]{:S(2)}) copy-start(bf16[576,576]{1,0:T(8,128)(2,1)S(1)} %all_gather.70) | copy-start | bytes 1990660
  99.7 86.8 %copy-start.63 = (f32[576]{0:T(1024)}, f32[576]{0:T(1024)S(1)}, u32[]{:S(2)}) copy-start(f32[576]{0:T(1024)S(1)} %convert_element_type.139) | copy-start | bytes 6916
  100.0 86.5 %copy-start.65 = (f32[1024]{0:T(1024)}, f32[1024]{0:T(1024)S(1)}, u32[]{:S(2)}) copy-start(f32[1024]{0:T(1024)S(1)} %add_rsqrt_fusion.1) | copy-start | bytes 12292
  102.9 38.5 %copy-start.7 = (f32[1024,64]{0,1:T(8,128)}, f32[1024,64]{0,1:T(8,128)S(1)}, u32[]{:S(2)}) copy-start(f32[1024,64]{0,1:T(8,128)S(1)} %get-tuple-element.157) | copy-start | bytes 786436
  102.9 38.6 %copy-start.5 = (f32[1024,64]{0,1:T(8,128)}, f32[1024,64]{0,1:T(8,128)S(1)}, u32[]{:S(2)}) copy-start(f32[1024,64]{0,1:T(8,128)S(1)} %get-tuple-element.156) | copy-start | bytes 786436
  104.0 38.1 %copy-start.23 = (bf16[512,192]{0,1:T(8,128)(2,1)}, bf16[512,192]{0,1:T(8,128)(2,1)S(1)}, u32[]{:S(2)}) copy-start(bf16[512,192]{0,1:T(8,128)(2,1)S(1)} %get-tuple-element.141) | copy-start | bytes 589828
  104.0 41.8 %copy-start.25 = (bf16[512,192]{0,1:T(8,128)(2,1)}, bf16[512,192]{0,1:T(8,128)(2,1)S(1)}, u32[]{:S(2)}) copy-start(bf16[512,192]{0,1:T(8,128)(2,1)S(1)} %get-tuple-element.144) | copy-start | bytes 589828
  104.0 83.9 %copy-start.44 = (bf16[512,192]{0,1:T(8,128)(2,1)}, bf16[512,192]{0,1:T(8,128)(2,1)S(1)}, u32[]{:S(2)}) copy-start(bf16[512,192]{0,1:T(8,128)(2,1)S(1)} %get-tuple-element.140) | copy-start | bytes 589828
  104.0 85.2 %copy-start.40 = (bf16[512,192]{0,1:T(8,128)(2,1)}, bf16[512,192]{0,1:T(8,128)(2,1)S(1)}, u32[]{:S(2)}) copy-start(bf16[512,192]{0,1:T(8,128)(2,1)S(1)} %get-tuple-element.143) | copy-start | bytes 589828
  104.0 86.5 %copy-start.46 = (bf16[512,192]{0,1:T(8,128)(2,1)}, bf16[512,192]{0,1:T(8,128)(2,1)S(1)}, u32[]{:S(2)}) copy-start(bf16[512,192]{0,1:T(8,128)(2,1)S(1)} %get-tuple-element.145) | copy-start | bytes 589828
  104.0 93.5 %copy-start.42 = (bf16[512,192]{0,1:T(8,128)(2,1)}, bf16[512,192]{0,1:T(8,128)(2,1)S(1)}, u32[]{:S(2)}) copy-start(bf16[512,192]{0,1:T(8,128)(2,1)S(1)} %get-tuple-element.142) | copy-start | bytes 589828
  142.1 55.5 %copy-start.11 = (bf16[1024,192]{0,1:T(8,128)(2,1)}, bf16[1024,192]{0,1:T(8,128)(2,1)S(1)}, u32[]{:S(2)}) copy-start(bf16[1024,192]{0,1:T(8,128)(2,1)S(1)} %fusion.115) | copy-start | bytes 1179652
  187.1 34.1 %copy-start.54 = (bf16[1024,192]{0,1:T(8,128)(2,1)}, bf16[1024,192]{0,1:T(8,128)(2,1)S(1)}, u32[]{:S(2)}) copy-start(bf16[1024,192]{0,1:T(8,128)(2,1)S(1)} %convolution_convert_fusion.1) | copy-start | bytes 1179652
  187.9 27.0 %copy-start.13 = (pred[512,1024]{0,1:T(8,128)(4,1)}, pred[512,1024]{0,1:T(8,128)(4,1)S(1)}, u32[]{:S(2)}) copy-start(pred[512,1024]{0,1:T(8,128)(4,1)S(1)} %get-tuple-element.171) | copy-start | bytes 1572868
  187.9 33.3 %copy-start.16 = (pred[512,1024]{0,1:T(8,128)(4,1)}, pred[512,1024]{0,1:T(8,128)(4,1)S(1)}, u32[]{:S(2)}) copy-start(pred[512,1024]{0,1:T(8,128)(4,1)S(1)} %get-tuple-element.170) | copy-start | bytes 1572868
  189.2 8.5 slice-start
  201.1 11.7 %copy-start = (f32[1024,512,3]{1,0,2:T(8,128)}, f32[1024,512,3]{1,0,2:T(8,128)S(1)}, u32[]{:S(2)}) copy-start(f32[1024,512,3]{1,0,2:T(8,128)S(1)} %get-tuple-element.178) | copy-start | bytes 18874372
  212.8 42.6 %copy-start.92 = (bf16[64,3,512]{2,0,1:T(8,128)(2,1)}, bf16[64,3,512]{2,0,1:T(8,128)(2,1)S(1)}, u32[]{:S(2)}) copy-start(bf16[64,3,512]{2,0,1:T(8,128)(2,1)S(1)} %fusion.66) | copy-start | bytes 589828
  214.9 40.5 %copy-start.94 = (bf16[64,3,512]{2,0,1:T(8,128)(2,1)}, bf16[64,3,512]{2,0,1:T(8,128)(2,1)S(1)}, u32[]{:S(2)}) copy-start(bf16[64,3,512]{2,0,1:T(8,128)(2,1)S(1)} %fusion.67) | copy-start | bytes 589828
  217.0 38.4 %copy-start.96 = (bf16[64,3,512]{2,0,1:T(8,128)(2,1)}, bf16[64,3,512]{2,0,1:T(8,128)(2,1)S(1)}, u32[]{:S(2)}) copy-start(bf16[64,3,512]{2,0,1:T(8,128)(2,1)S(1)} %fusion.68) | copy-start | bytes 589828
  219.0 36.3 %copy-start.98 = (bf16[64,3,512]{2,0,1:T(8,128)(2,1)}, bf16[64,3,512]{2,0,1:T(8,128)(2,1)S(1)}, u32[]{:S(2)}) copy-start(bf16[64,3,512]{2,0,1:T(8,128)(2,1)S(1)} %fusion.69) | copy-start | bytes 589828
  221.1 34.3 %copy-start.100 = (bf16[64,3,512]{2,0,1:T(8,128)(2,1)}, bf16[64,3,512]{2,0,1:T(8,128)(2,1)S(1)}, u32[]{:S(2)}) copy-start(bf16[64,3,512]{2,0,1:T(8,128)(2,1)S(1)} %fusion.70) | copy-start | bytes 589828
  223.2 33.3 %copy-start.101 = (bf16[64,3,512]{2,0,1:T(8,128)(2,1)}, bf16[64,3,512]{2,0,1:T(8,128)(2,1)S(1)}, u32[]{:S(2)}) copy-start(bf16[64,3,512]{2,0,1:T(8,128)(2,1)S(1)} %fusion.71) | copy-start | bytes 589828
  256.5 33.3 %copy-start.3 = (f32[1024,576]{0,1:T(8,128)}, f32[1024,576]{0,1:T(8,128)S(1)}, u32[]{:S(2)}) copy-start(f32[1024,576]{0,1:T(8,128)S(1)} %get-tuple-element.183) | copy-start | bytes 7077892
  266.3 7.2 copy-start.30
  273.6 10.5 copy-start.88
  291.0 8.9 slice-start.6
  292.4 45.9 %copy-start.48 = (bf16[512,192]{0,1:T(8,128)(2,1)}, bf16[512,192]{0,1:T(8,128)(2,1)S(1)}, u32[]{:S(2)}) copy-start(bf16[512,192]{0,1:T(8,128)(2,1)S(1)} %get-tuple-element.136) | copy-start | bytes 589828
  292.4 49.6 %copy-start.50 = (bf16[512,192]{0,1:T(8,128)(2,1)}, bf16[512,192]{0,1:T(8,128)(2,1)S(1)}, u32[]{:S(2)}) copy-start(bf16[512,192]{0,1:T(8,128)(2,1)S(1)} %get-tuple-element.135) | copy-start | bytes 589828
  292.4 53.2 %copy-start.56 = (bf16[512,192]{0,1:T(8,128)(2,1)}, bf16[512,192]{0,1:T(8,128)(2,1)S(1)}, u32[]{:S(2)}) copy-start(bf16[512,192]{0,1:T(8,128)(2,1)S(1)} %get-tuple-element.137) | copy-start | bytes 589828
  292.4 7.5 slice-start.7
  319.7 12.4 %copy-start.12 = (bf16[1024,192]{0,1:T(8,128)(2,1)S(1)}, bf16[1024,192]{0,1:T(8,128)(2,1)}, u32[]{:S(2)}) copy-start(bf16[1024,192]{0,1:T(8,128)(2,1)} %copy-done.11) | copy-start | bytes 1179652
  336.5 9.1 slice-start.2
  338.3 7.3 slice-start.3
  382.7 126.4 %reduce-scatter.27.cloned.1.call-start = ((), (), s32[]{:S(2)}) async-start(), calls=%async_computation.17 | async-start | bytes 663552 | tf_op jit(solution)/shard_map/reduce_scatter | solution.py:317
  383.7 9.2 slice-start.8
  395.7 178.3 %reduce-scatter.29.cloned.1.call-start = ((), (), s32[]{:S(2)}) async-start(), calls=%async_computation.18 | async-start | bytes 663552 | tf_op jit(solution)/shard_map/reduce_scatter | solution.py:318
  402.5 238.0 %reduce-scatter.53.cloned.1.call-start = ((), (), s32[]{:S(2)}) async-start(), calls=%async_computation.30 | async-start | bytes 1658880
  406.9 315.8 %reduce-scatter.31.cloned.1.call-start = ((), (), s32[]{:S(2)}) async-start(), calls=%async_computation.19 | async-start | bytes 3981312 | tf_op jit(solution)/shard_map/reduce_scatter | solution.py:320
  412.6 392.8 %reduce-scatter.35.cloned.1.call-start = ((), (), s32[]{:S(2)}) async-start(), calls=%async_computation.21 | async-start | bytes 3981312 | tf_op jit(solution)/shard_map/reduce_scatter | solution.py:321
  418.4 469.6 %reduce-scatter.39.cloned.1.call-start = ((), (), s32[]{:S(2)}) async-start(), calls=%async_computation.23 | async-start | bytes 3981312 | tf_op jit(solution)/shard_map/reduce_scatter | solution.py:322
  425.3 297.4 %copy-start.102 = (u32[32]{0:T(128)S(1)}, u32[32]{0:T(128)}, u32[]{:S(2)}) copy-start(u32[32]{0:T(128)} %constant.103) | copy-start | bytes 388
  425.3 298.7 %copy-start.39 = (bf16[1024,576]{0,1:T(8,128)(2,1)S(1)}, bf16[1024,576]{0,1:T(8,128)(2,1)}, u32[]{:S(2)}) copy-start(bf16[1024,576]{0,1:T(8,128)(2,1)} %copy-done.38) | copy-start | bytes 3538948
  425.4 501.3 %reduce-scatter.43.cloned.1.call-start = ((), (), s32[]{:S(2)}) async-start(), calls=%async_computation.25 | async-start | bytes 368640
  446.0 486.9 %reduce-scatter.45.cloned.1.call-start = ((), (), s32[]{:S(2)}) async-start(), calls=%async_computation.26 | async-start | bytes 122880
  510.7 444.8 %reduce-scatter.47.cloned.1.call-start = ((), (), s32[]{:S(2)}) async-start(), calls=%async_computation.27 | async-start | bytes 122880
  575.7 403.0 %reduce-scatter.49.cloned.1.call-start = ((), (), s32[]{:S(2)}) async-start(), calls=%async_computation.28 | async-start | bytes 368640
  642.3 360.5 %reduce-scatter.33.cloned.1.call-start = ((), (), s32[]{:S(2)}) async-start(), calls=%async_computation.20 | async-start | bytes 552960 | tf_op jit(solution)/shard_map/reduce_scatter | solution.py:333
  722.7 304.1 %reduce-scatter.37.cloned.1.call-start = ((), (), s32[]{:S(2)}) async-start(), calls=%async_computation.22 | async-start | bytes 552960 | tf_op jit(solution)/shard_map/reduce_scatter | solution.py:334
  724.0 81.5 %copy-start.29 = (bf16[1024,192]{0,1:T(8,128)(2,1)S(1)}, bf16[1024,192]{0,1:T(8,128)(2,1)}, u32[]{:S(2)}) copy-start(bf16[1024,192]{0,1:T(8,128)(2,1)} %copy-done.28) | copy-start | bytes 1179652
  724.0 81.5 %copy-start.33 = (bf16[576,192]{1,0:T(8,128)(2,1)S(1)}, bf16[576,192]{1,0:T(8,128)(2,1)}, u32[]{:S(2)}) copy-start(bf16[576,192]{1,0:T(8,128)(2,1)} %copy-done.32) | copy-start | bytes 663556
  727.7 78.3 %copy-start.35 = (bf16[576,192]{1,0:T(8,128)(2,1)S(1)}, bf16[576,192]{1,0:T(8,128)(2,1)}, u32[]{:S(2)}) copy-start(bf16[576,192]{1,0:T(8,128)(2,1)} %copy-done.34) | copy-start | bytes 663556
  727.7 78.3 %copy-start.60 = (bf16[1024,64]{0,1:T(8,128)(2,1)S(1)}, bf16[1024,64]{0,1:T(8,128)(2,1)}, u32[]{:S(2)}) copy-start(bf16[1024,64]{0,1:T(8,128)(2,1)} %fusion.108) | copy-start | bytes 393220
  727.7 78.3 %copy-start.62 = (bf16[1024,64]{0,1:T(8,128)(2,1)S(1)}, bf16[1024,64]{0,1:T(8,128)(2,1)}, u32[]{:S(2)}) copy-start(bf16[1024,64]{0,1:T(8,128)(2,1)} %copy-done.61) | copy-start | bytes 393220
  805.5 245.5 %reduce-scatter.41.cloned.1.call-start = ((), (), s32[]{:S(2)}) async-start(), calls=%async_computation.24 | async-start | bytes 552960 | tf_op jit(solution)/shard_map/reduce_scatter | solution.py:335
  888.0 33.0 %copy-start.87 = (bf16[1536,576]{0,1:T(8,128)(2,1)S(1)}, bf16[1536,576]{0,1:T(8,128)(2,1)}, u32[]{:S(2)}) copy-start(bf16[1536,576]{0,1:T(8,128)(2,1)} %all-gather.8.cloned.1.call-done) | copy-start | bytes 5308420
  (79 other events, 222.7 us)
Sparse Core Ops, SparseCore 0:
  16.3 55.7 all-gather.3
  74.3 46.6 all-gather.5
  123.2 47.4 all-gather.7
  382.8 61.2 reduce-scatter.50
  447.3 61.7 reduce-scatter.26
  512.2 61.7 reduce-scatter.28
  577.5 62.9 reduce-scatter.52
  644.1 78.5 reduce-scatter.30
  726.3 79.0 reduce-scatter.34
  808.9 79.0 reduce-scatter.38
  890.5 19.8 reduce-scatter.42
  913.2 19.6 reduce-scatter.44
  935.9 19.6 reduce-scatter.46
  958.5 20.2 reduce-scatter.48
  981.6 21.0 reduce-scatter.32
  1005.7 21.0 reduce-scatter.36
  1029.8 21.0 reduce-scatter.40
where the time goes:
time: 1070 us; the launch traced here: 1060 us
  waiting for transfers between devices  569 us (53%)
  blocking collectives  221 us (21%)
  matrix products  174 us (16%)
  other arithmetic  46.6 us (4%)
  local copies, waits for them, and re-layouts  29.1 us (3%)
  between operations  17.4 us (2%)
    unnamed x23, waiting for transfers between devices  134 us
    reduce_scatter x1, waiting for transfers between devices, on_device(): lax.psum_scatter(grad_gate, 'fsdp', scatter_dimension=0, tiled=True)  80.3 us
    reduce_scatter x1, waiting for transfers between devices, on_device(): lax.psum_scatter(grad_down, 'fsdp', scatter_dimension=1, tiled=True)  78.5 us
    reduce_scatter x1, waiting for transfers between devices, on_device(): lax.psum_scatter(grad_up, 'fsdp', scatter_dimension=0, tiled=True)  77.7 us
    reduce_scatter x1, waiting for transfers between devices, on_device(): lax.psum_scatter(grad_value, 'fsdp', scatter_dimension=0, tiled=True)  63.3 us
    reduce_scatter x1, waiting for transfers between devices, on_device(): lax.psum_scatter(grad_key, 'fsdp', scatter_dimension=0, tiled=True)  63.1 us
    unnamed x3, blocking collectives  47.5 us
    dot_general x6, matrix products, attend_backward(): jnp.einsum('qgd,td->gqt', grad_block, value_head, preferred_element_type=...  39.1 us
  transfers between devices with their start and end apart: 17, of which 13 were waited for; matrix products, arithmetic and copies ran while one was open for 13% of the time, Pallas kernels for 0%

commit v1 on v0

--- a/solution.py
+++ b/solution.py
@@ -52,14 +52,15 @@
     group_size = Q_HEADS // KV_HEADS
     first_row = block_index * QBLOCK
     row_index = first_row + jnp.arange(QBLOCK, dtype=jnp.int32)
-    col_index = jnp.arange(LEN, dtype=jnp.int32)
+    last_col = first_row + QBLOCK
+    col_index = jnp.arange(last_col, dtype=jnp.int32)
     seg_block = segment[first_row : first_row + QBLOCK]
-    allowed = (col_index[None, :] <= row_index[:, None]) & (segment[None, :] == seg_block[:, None])
+    allowed = (col_index[None, :] <= row_index[:, None]) & (segment[None, :last_col] == seg_block[:, None])
     width = group_size * HEAD_DIM
     query_block = queries[
         first_row : first_row + QBLOCK, kv_head * width : (kv_head + 1) * width
     ].reshape(QBLOCK, group_size, HEAD_DIM)
-    key_head = keys[:, kv_head * HEAD_DIM : (kv_head + 1) * HEAD_DIM]
+    key_head = keys[:last_col, kv_head * HEAD_DIM : (kv_head + 1) * HEAD_DIM]
     scores = jnp.einsum(
         "qgd,td->gqt", query_block, key_head, preferred_element_type=jnp.float32
     ) * HEAD_DIM ** (-0.5)
@@ -80,7 +81,7 @@
             expo = jnp.exp(scores - top_value)
             total = jnp.sum(expo, axis=-1, keepdims=True)
             probability = (expo / total).astype(jnp.bfloat16)
-            value_head = values[:, kv_head * HEAD_DIM : (kv_head + 1) * HEAD_DIM]
+            value_head = values[: (block_index + 1) * QBLOCK, kv_head * HEAD_DIM : (kv_head + 1) * HEAD_DIM]
             attended = jnp.einsum(
                 "gqt,td->qgd", probability, value_head, preferred_element_type=jnp.float32
             )
@@ -99,8 +100,8 @@
     group_size = Q_HEADS // KV_HEADS
     scale = HEAD_DIM ** (-0.5)
     width = group_size * HEAD_DIM
-    grad_key_heads = [jnp.zeros((LEN, HEAD_DIM), jnp.float32) for kv_head in range(KV_HEADS)]
-    grad_value_heads = [jnp.zeros((LEN, HEAD_DIM), jnp.float32) for kv_head in range(KV_HEADS)]
+    grad_key_heads = [None] * KV_HEADS
+    grad_value_heads = [None] * KV_HEADS
     block_rows = []
     for block_index in range(LEN // QBLOCK):
         first_row = block_index * QBLOCK
@@ -112,15 +113,18 @@
             expo = jnp.exp(scores - tops[block_index, kv_head])
             prob_full = expo / totals[block_index, kv_head]
             probability = prob_full.astype(jnp.bfloat16)
-            value_head = values[:, kv_head * HEAD_DIM : (kv_head + 1) * HEAD_DIM]
+            value_head = values[: (block_index + 1) * QBLOCK, kv_head * HEAD_DIM : (kv_head + 1) * HEAD_DIM]
             grad_block = grad_mixture[
                 first_row : first_row + QBLOCK, kv_head * width : (kv_head + 1) * width
             ].reshape(QBLOCK, group_size, HEAD_DIM)
             grad_probs = jnp.einsum(
                 "qgd,td->gqt", grad_block, value_head, preferred_element_type=jnp.float32
             )
-            grad_value_heads[kv_head] = grad_value_heads[kv_head] + jnp.einsum(
-                "gqt,qgd->td", probability, grad_block, preferred_element_type=jnp.float32
+            grad_value_heads[kv_head] = add_rows(
+                grad_value_heads[kv_head],
+                jnp.einsum(
+                    "gqt,qgd->td", probability, grad_block, preferred_element_type=jnp.float32
+                ),
             )
             delta = jnp.sum(prob_full * grad_probs, axis=-1, keepdims=True)
             grad_scores = (prob_full * (grad_probs - delta)).astype(jnp.bfloat16)
@@ -128,12 +132,12 @@
                 jnp.einsum("gqt,td->qgd", grad_scores, key_head, preferred_element_type=jnp.float32)
                 * scale
             )
-            grad_key_heads[kv_head] = (
-                grad_key_heads[kv_head]
-                + jnp.einsum(
+            grad_key_heads[kv_head] = add_rows(
+                grad_key_heads[kv_head],
+                jnp.einsum(
                     "gqt,qgd->td", grad_scores, query_block, preferred_element_type=jnp.float32
                 )
-                * scale
+                * scale,
             )
             head_rows.append(grad_query_block.reshape(QBLOCK, width))
         block_rows.append(jnp.concatenate(head_rows, axis=1))
@@ -143,6 +147,59 @@
         jnp.concatenate(grad_key_heads, axis=1),
         jnp.concatenate(grad_value_heads, axis=1),
     )
+
+
+def add_rows(longest, shorter):
+    if longest is None:
+        return shorter
+    rows = longest.shape[0]
+    return jnp.concatenate([shorter[:rows] + longest, shorter[rows:]], axis=0)
+
+
+def pack_columns(parts):
+    width = sum(part.shape[-1] for part in parts)
+    packed = jnp.concatenate(parts, axis=-1)
+    return jnp.pad(packed, [(0, 0)] * (packed.ndim - 1) + [(0, -width % 128)])
+
+
+def gather_pack(packed):
+    rows = lax.all_gather(packed, "fsdp", axis=0, tiled=True)
+    return lax.all_gather(rows, "dp", axis=0, tiled=False)
+
+
+def split_columns(packed, widths):
+    parts, start = ([], 0)
+    for width in widths:
+        parts.append(packed[..., start : start + width])
+        start += width
+    return parts
+
+
+def split_full(packed, widths):
+    pieces = packed.shape[0]
+    return [
+        part[0]
+        if width == 1
+        else jnp.concatenate([part[piece] for piece in range(pieces)], axis=1)
+        for part, width in zip(split_columns(packed, widths), widths)
+    ]
+
+
+def reduce_pack(matrices, vectors, model_part):
+    pieces = lax.axis_size("dp")
+    blocks = []
+    for piece in range(pieces):
+        columns = []
+        for matrix in matrices:
+            width = matrix.shape[1] // pieces
+            columns.append(matrix[:, piece * width : (piece + 1) * width])
+        blocks.append(pack_columns(columns + list(vectors)).astype(jnp.bfloat16))
+    sent = jnp.stack(blocks)
+    got = lax.all_to_all(sent, "dp", 0, 0, tiled=True)
+    half = jnp.sum(got.astype(jnp.float32), axis=0)
+    shares = half.reshape(half.shape[0] // model_part, model_part, half.shape[1])
+    shares = lax.all_to_all(shares.astype(jnp.bfloat16), "fsdp", 0, 0, tiled=True)
+    return jnp.sum(shares.astype(jnp.float32), axis=0)
 
 
 def on_device(
@@ -160,25 +217,29 @@
     w_down,
     cotangent,
 ):
-    columns = (
-        lax.all_gather(w_query, "dp", axis=1, tiled=True),
-        lax.all_gather(w_key, "dp", axis=1, tiled=True),
-        lax.all_gather(w_value, "dp", axis=1, tiled=True),
-        lax.all_gather(w_output, "dp", axis=0, tiled=True),
-        lax.all_gather(w_gate, "dp", axis=1, tiled=True),
-        lax.all_gather(w_up, "dp", axis=1, tiled=True),
-        lax.all_gather(w_down, "dp", axis=0, tiled=True),
-    )
+    model_part = attn_gain.shape[0]
+    attn_widths = (w_query.shape[1], w_output.shape[0], w_key.shape[1], w_value.shape[1], 1, 1)
+    mlp_widths = (w_gate.shape[1], w_up.shape[1], w_down.shape[0])
+    attn_pack = pack_columns(
+        (w_query, w_output.T, w_key, w_value, attn_gain[:, None], mlp_gain[:, None])
+    )
+    mlp_pack = pack_columns((w_gate, w_up, w_down.T))
+    attn_all = gather_pack(attn_pack)
+    mlp_all = gather_pack(mlp_pack)
+    full_query, full_output, full_key, full_value, gains_attn, gains_mlp = split_full(
+        attn_all, attn_widths
+    )
+    full_gate, full_up, full_down = split_full(mlp_all, mlp_widths)
     weights = (
-        lax.all_gather(attn_gain, "fsdp", axis=0, tiled=True),
-        lax.all_gather(mlp_gain, "fsdp", axis=0, tiled=True),
-        lax.all_gather(columns[0], "fsdp", axis=0, tiled=True),
-        lax.all_gather(columns[1], "fsdp", axis=0, tiled=True),
-        lax.all_gather(columns[2], "fsdp", axis=0, tiled=True),
-        lax.all_gather(columns[3], "fsdp", axis=1, tiled=True),
-        lax.all_gather(columns[4], "fsdp", axis=0, tiled=True),
-        lax.all_gather(columns[5], "fsdp", axis=0, tiled=True),
-        lax.all_gather(columns[6], "fsdp", axis=1, tiled=True),
+        gains_attn[:, 0],
+        gains_mlp[:, 0],
+        full_query,
+        full_key,
+        full_value,
+        full_output,
+        full_gate,
+        full_up,
+        full_down,
     )
     row_count = tokens.shape[0]
     seq_count = segments.shape[0]
@@ -207,38 +268,19 @@
     seq_values = values.reshape(seq_count, LEN, KVW)
     mixture, tops, totals = lax.map(attend_forward, (seq_queries, seq_keys, seq_values, segments))
     mixture = mixture.reshape(row_count, QW)
-    resid = inputs + jnp.dot(mixture, weights[5], preferred_element_type=jnp.float32)
+    resid = inputs + jnp.einsum("rq,dq->rd", mixture, weights[5], preferred_element_type=jnp.float32)
     scaled_mlp, inverse_mlp = norm_rows(resid)
     normed_mlp = (scaled_mlp * gain_mlp).astype(jnp.bfloat16)
     gate_pre = jnp.dot(normed_mlp, weights[6], preferred_element_type=jnp.float32)
     up_pre = jnp.dot(normed_mlp, weights[7], preferred_element_type=jnp.float32)
     hidden = (jax.nn.silu(gate_pre) * up_pre).astype(jnp.bfloat16)
-    output = (resid + jnp.dot(hidden, weights[8], preferred_element_type=jnp.float32)).astype(
+    output = (resid + jnp.einsum("rf,df->rd", hidden, weights[8], preferred_element_type=jnp.float32)).astype(
         jnp.bfloat16
     )
-    again = (
-        lax.all_gather(w_query, "dp", axis=1, tiled=True),
-        lax.all_gather(w_key, "dp", axis=1, tiled=True),
-        lax.all_gather(w_value, "dp", axis=1, tiled=True),
-        lax.all_gather(w_output, "dp", axis=0, tiled=True),
-        lax.all_gather(w_gate, "dp", axis=1, tiled=True),
-        lax.all_gather(w_up, "dp", axis=1, tiled=True),
-        lax.all_gather(w_down, "dp", axis=0, tiled=True),
-    )
-    back_weights = (
-        lax.all_gather(attn_gain, "fsdp", axis=0, tiled=True),
-        lax.all_gather(mlp_gain, "fsdp", axis=0, tiled=True),
-        lax.all_gather(again[0], "fsdp", axis=0, tiled=True),
-        lax.all_gather(again[1], "fsdp", axis=0, tiled=True),
-        lax.all_gather(again[2], "fsdp", axis=0, tiled=True),
-        lax.all_gather(again[3], "fsdp", axis=1, tiled=True),
-        lax.all_gather(again[4], "fsdp", axis=0, tiled=True),
-        lax.all_gather(again[5], "fsdp", axis=0, tiled=True),
-        lax.all_gather(again[6], "fsdp", axis=1, tiled=True),
-    )
-    grad_down = jnp.einsum("rf,rd->fd", hidden, cotangent, preferred_element_type=jnp.float32)
+    back_weights = weights
+    grad_down = jnp.einsum("rd,rf->df", cotangent, hidden, preferred_element_type=jnp.float32)
     grad_hidden = jnp.einsum(
-        "rd,fd->rf", cotangent, back_weights[8], preferred_element_type=jnp.float32
+        "rd,df->rf", cotangent, back_weights[8], preferred_element_type=jnp.float32
     )
     sigmoid = jax.nn.sigmoid(gate_pre)
     grad_gate_pre = (grad_hidden * up_pre * sigmoid * (1.0 + gate_pre * (1.0 - sigmoid))).astype(
@@ -260,9 +302,9 @@
         grad_normed_mlp * back_weights[1].astype(jnp.float32), scaled_mlp, inverse_mlp
     )
     grad_branch = grad_resid.astype(jnp.bfloat16)
-    grad_output = jnp.einsum("rq,rd->qd", mixture, grad_branch, preferred_element_type=jnp.float32)
+    grad_output = jnp.einsum("rd,rq->dq", grad_branch, mixture, preferred_element_type=jnp.float32)
     grad_mixture = jnp.einsum(
-        "rd,qd->rq", grad_branch, back_weights[5], preferred_element_type=jnp.float32
+        "rd,dq->rq", grad_branch, back_weights[5], preferred_element_type=jnp.float32
     ).astype(jnp.bfloat16)
     grad_queries, grad_keys, grad_values = lax.map(
         attend_backward,
@@ -309,43 +351,28 @@
     grad_tokens = grad_resid + norm_back(
         grad_normed_attn * back_weights[0].astype(jnp.float32), scaled_attn, inverse_attn
     )
-    replicas = lax.axis_size("dp")
-    first_sums = (
-        lax.psum_scatter(grad_attn_gain, "fsdp", scatter_dimension=0, tiled=True),
-        lax.psum_scatter(grad_mlp_gain, "fsdp", scatter_dimension=0, tiled=True),
-        lax.psum_scatter(grad_query, "fsdp", scatter_dimension=0, tiled=True),
-        lax.psum_scatter(grad_key, "fsdp", scatter_dimension=0, tiled=True),
-        lax.psum_scatter(grad_value, "fsdp", scatter_dimension=0, tiled=True),
-        lax.psum_scatter(grad_output, "fsdp", scatter_dimension=1, tiled=True),
-        lax.psum_scatter(grad_gate, "fsdp", scatter_dimension=0, tiled=True),
-        lax.psum_scatter(grad_up, "fsdp", scatter_dimension=0, tiled=True),
-        lax.psum_scatter(grad_down, "fsdp", scatter_dimension=1, tiled=True),
-    )
-    spread_attn = jnp.broadcast_to(first_sums[0][:, None], (first_sums[0].shape[0], replicas))
-    spread_mlp = jnp.broadcast_to(first_sums[1][:, None], (first_sums[1].shape[0], replicas))
-    final_sums = (
-        lax.psum_scatter(spread_attn, "dp", scatter_dimension=1, tiled=True),
-        lax.psum_scatter(spread_mlp, "dp", scatter_dimension=1, tiled=True),
-        lax.psum_scatter(first_sums[2], "dp", scatter_dimension=1, tiled=True),
-        lax.psum_scatter(first_sums[3], "dp", scatter_dimension=1, tiled=True),
-        lax.psum_scatter(first_sums[4], "dp", scatter_dimension=1, tiled=True),
-        lax.psum_scatter(first_sums[5], "dp", scatter_dimension=0, tiled=True),
-        lax.psum_scatter(first_sums[6], "dp", scatter_dimension=1, tiled=True),
-        lax.psum_scatter(first_sums[7], "dp", scatter_dimension=1, tiled=True),
-        lax.psum_scatter(first_sums[8], "dp", scatter_dimension=0, tiled=True),
+    mlp_sum = reduce_pack((grad_gate, grad_up, grad_down), (), model_part)
+    attn_sum = reduce_pack(
+        (grad_query, grad_output, grad_key, grad_value),
+        (grad_attn_gain[:, None], grad_mlp_gain[:, None]),
+        model_part,
+    )
+    own_gate, own_up, own_down = split_columns(mlp_sum, mlp_widths)
+    own_query, own_output, own_key, own_value, own_attn_gain, own_mlp_gain = split_columns(
+        attn_sum, attn_widths
     )
     return (
         output,
         grad_tokens,
-        final_sums[0][:, 0],
-        final_sums[1][:, 0],
-        final_sums[2],
-        final_sums[3],
-        final_sums[4],
-        final_sums[5],
-        final_sums[6],
-        final_sums[7],
-        final_sums[8],
+        own_attn_gain[:, 0],
+        own_mlp_gain[:, 0],
+        own_query,
+        own_key,
+        own_value,
+        own_output.T,
+        own_gate,
+        own_up,
+        own_down.T,
     )
 
 

time: 1070 us -> 453 us (0.42)
  waiting for transfers between devices: 569 us -> 147 us
  blocking collectives: 221 us -> 37 us
  matrix products: 174 us -> 128 us
  local copies, waits for them, and re-layouts: 29.1 us -> 52.7 us
  starting transfers between devices: 0.95 us -> 18.6 us
    reduce_scatter x8 -> x0, waiting for transfers between devices: 435 us -> none  [the longest x1 80.3 us: on_device(): lax.psum_scatter(grad_gate, 'fsdp', scatter_dimension=0, tiled=True)]
    all_gather x11 -> x1, blocking collectives: 173 us -> 37 us  [gather_pack(): rows = lax.all_gather(packed, 'fsdp', axis=0, tiled=True)]
    unnamed x23 -> x3, waiting for transfers between devices: 134 us -> 0.05 us
    all_to_all x0 -> x4, waiting for transfers between devices: none -> 111 us  [the longest x2 81.3 us: reduce_pack(): got = lax.all_to_all(sent, 'dp', 0, 0, tiled=True)]
    unnamed x3 -> x0, blocking collectives: 47.5 us -> none
    all_gather x3, waiting for transfers between devices: 0.02 us -> 35.6 us  [the longest x2 31 us: gather_pack(): return lax.all_gather(rows, 'dp', axis=0, tiled=False)]
    concatenate x0 -> x7, local copies, waits for them, and re-layouts: none -> 18.7 us  [pack_columns(): packed = jnp.concatenate(parts, axis=-1)]
    all_to_all x0 -> x4, starting transfers between devices: none -> 18.5 us  [the longest x2 9.79 us: reduce_pack(): lax.all_to_all(shares.astype(jnp.bfloat16), 'fsdp', 0, 0, tiled=True)]
  transfers between devices with their start and end apart: 17 -> 7, of which waited for: 13 -> 7; matrix products, arithmetic and copies ran while one was open for 13% -> 15% of each run, Pallas kernels for 0% -> 0%
where the time goes in v1:
time: 453 us; the launch traced here: 448 us
  waiting for transfers between devices  147 us (32%)
  matrix products  128 us (28%)
  local copies, waits for them, and re-layouts  52.7 us (12%)
  other arithmetic  49.4 us (11%)
  blocking collectives  37 us (8%)
  starting transfers between devices  18.6 us (4%)
  between operations  16.1 us (4%)
    all_to_all x2, waiting for transfers between devices, reduce_pack(): got = lax.all_to_all(sent, 'dp', 0, 0, tiled=True)  81.3 us
    all_gather x1, blocking collectives, gather_pack(): rows = lax.all_gather(packed, 'fsdp', axis=0, tiled=True)  37 us
    all_gather x2, waiting for transfers between devices, gather_pack(): return lax.all_gather(rows, 'dp', axis=0, tiled=False)  31 us
    all_to_all x2, waiting for transfers between devices, reduce_pack(): lax.all_to_all(shares.astype(jnp.bfloat16), 'fsdp', 0, 0, tiled=True)  29.7 us
    dot_general x6, matrix products, attend_backward(): jnp.einsum('qgd,td->gqt', grad_block, value_head, preferred_element_type=...  23.9 us
    concatenate x7, local copies, waits for them, and re-layouts, pack_columns(): packed = jnp.concatenate(parts, axis=-1)  18.7 us
    convert_element_type x2, other arithmetic, attend_backward(): grad_scores = (prob_full * (grad_probs - delta)).astype(jnp.bfloat16)  16.9 us
    dot_general x1, matrix products, on_device(): up_pre = jnp.dot(normed_mlp, weights[7], preferred_element_type=jnp.float32)  15.3 us
  transfers between devices with their start and end apart: 7, of which 7 were waited for; matrix products, arithmetic and copies ran while one was open for 15% of the time, Pallas kernels for 0%

profile of v1, /device:TPU:0, one launch (start us, length us, event | category | flops | bytes accessed | tf_op | source)
XLA Modules:
  0.0 448.3 jit_solution(15792611575711188905)
XLA Ops:
  7.2 1.6 pad_maximum_fusion.17
  13.9 37.0 %all_gather.18 = bf16[576,512]{1,0:T(8,128)(2,1)} all-gather(bf16[72,512]{1,0:T(8,128)(2,1)S(1)} %pad.21), channel_id=1, replica_groups=mesh['dp'=4,'fsdp'=8] {'fsdp'}, dimensions={0}, use_global_device_ids=true | all-gather | bytes 663552 | tf_op jit(solution)/shard_map/all_gather | solution.py:166
  53.7 4.6 %all-gather.6.cloned.1.call-done = bf16[576,1152]{1,0:T(8,128)(2,1)} async-done(((bf16[72,1152]{1,0:T(8,128)(2,1)}), bf16[576,1152]{1,0:T(8,128)(2,1)}) %all-gather.6.cloned.1.call-update) | async-done | bytes 1327120 | tf_op jit(solution)/shard_map/all_gather | solution.py:166
  58.4 24.7 %all-gather.8.cloned.1.call-done = bf16[2304,512]{1,0:T(8,128)(2,1)} async-done(((bf16[576,512]{1,0:T(8,128)(2,1)}), bf16[2304,512]{1,0:T(8,128)(2,1)}) %all-gather.8.cloned.1.call-update) | async-done | bytes 2359312 | tf_op jit(solution)/shard_map/all_gather | solution.py:167
  83.1 1.4 convert_reduce_fusion.2
  84.5 1.8 slice_bitcast_fusion.39
  86.3 1.6 slice_bitcast_fusion.27
  89.0 1.6 fusion.165
  94.7 1.3 fusion.17
  96.0 1.8 fusion.43
  97.9 1.6 fusion.44
  99.5 3.3 fusion.14
  102.8 2.7 fusion.15
  109.9 2.0 fusion.74
  112.0 2.0 fusion.73
  114.1 2.0 fusion.75
  116.3 1.2 multiply_reduce_fusion.2
  119.1 6.3 %all-gather.10.cloned.1.call-done = bf16[2304,1152]{1,0:T(8,128)(2,1)} async-done(((bf16[576,1152]{1,0:T(8,128)(2,1)}), bf16[2304,1152]{1,0:T(8,128)(2,1)}) %all-gather.10.cloned.1.call-update) | async-done | bytes 5308432 | tf_op jit(solution)/shard_map/all_gather | solution.py:167
  125.4 3.1 slice_bitcast_fusion.15
  128.6 15.3 %fusion.129 = f32[1024,1536]{1,0:T(8,128)S(1)} fusion(bf16[1024,576]{0,1:T(8,128)(2,1)S(1)} %multiply_convert_fusion.1, bf16[576,384]{1,0:T(8,128)(2,1)S(1)} %get-tuple-element.187, bf16[576,384]{1,0:T(8,128)(2,1)S(1)} %get-tuple-element.188, bf16[576,384]{1,0:T(8,128)(2,1)S(1)} %get-tuple-element.189, bf16[576,384]{1,0:T(8,128)(2,1)S(1)} %get-tuple-element.190), kind=kOutput, calls=%fused_computation.234 | convolution fusion | flops 1819017216 | bytes 9240576 | tf_op jit(solution)/shard_map/dot_general | solution.py:275
  143.9 5.0 %fusion.131 = f32[1024,1536]{1,0:T(8,128)} fusion(bf16[1024,576]{0,1:T(8,128)(2,1)S(1)} %multiply_convert_fusion.1, bf16[576,384]{1,0:T(8,128)(2,1)S(1)} %get-tuple-element.191, bf16[576,384]{1,0:T(8,128)(2,1)S(1)} %get-tuple-element.192, bf16[576,384]{1,0:T(8,128)(2,1)S(1)} %get-tuple-element.193, bf16[576,384]{1,0:T(8,128)(2,1)S(1)} %get-tuple-element.194), kind=kOutput, calls=%fused_computation.236 | convolution fusion | flops 1819017216 | bytes 9240576 | tf_op jit(solution)/shard_map/dot_general | solution.py:274
  149.0 9.5 %fusion.12 = (bf16[1024,1536]{1,0:T(8,128)(2,1)S(1)}, bf16[1024,1536]{1,0:T(8,128)(2,1)}, bf16[1024,1536]{1,0:T(8,128)(2,1)}) fusion(f32[1024,1536]{1,0:T(8,128)} %fusion.131, f32[1024,1536]{1,0:T(8,128)S(1)} %fusion.129, bf16[1024,576]{0,1:T(8,128)(2,1)S(1)} %copy-done.35, bf16[576,384]{1,0:T(8,128)(2,1)S(1)} %get-tuple-element.184, ...), kind=kOutput, calls=%fused_computation.20 | convolution fusion | flops 1842610176 | bytes 24969216 | tf_op jit(solution)/shard_map/rd,df->rf/dot_general | solution.py:282
  158.5 4.1 fusion.130
  162.5 3.2 convolution_convert_fusion.2
  165.8 3.2 convolution_convert_fusion.1
  169.0 3.1 multiply_reduce_fusion
  175.5 1.5 convolution_convert_fusion.3
  177.7 3.7 fusion.136
  181.4 3.6 fusion.138
  185.1 2.8 fusion.82
  187.9 3.1 fusion.79
  191.1 2.7 fusion.76
  193.8 11.3 %fusion.6 = (f32[3,512]{1,0:T(4,128)S(1)}, f32[3,512]{1,0:T(4,128)S(1)}, f32[3,512]{1,0:T(4,128)S(1)}, f32[1024,512,3]{1,0,2:T(8,128)}) fusion(f32[3,512]{1,0:T(4,128)S(1)} %copy-done.106, f32[3,512]{1,0:T(4,128)S(1)} %copy-done.107, f32[1024,512,3]{1,0,2:T(8,128)} %copy-done.16, pred[512,1024]{0,1:T(8,128)(4,1)S(1)} %copy-done.19, ...), kind=kOutput, calls=%fused_computation.12 | convolution fusion | flops 229633536 | bytes 38668288 | tf_op jit(solution)/shard_map/while/body/eval_jaxpr/qgd,td->gqt/dot_general | solution.py:120
  205.1 12.3 %fusion.8 = (bf16[3,512,1024]{1,2,0:T(8,128)(2,1)S(1)}, bf16[3,512,1024]{1,2,0:T(8,128)(2,1)S(1)}, bf16[3,512,1024]{1,2,0:T(8,128)(2,1)S(1)}) fusion(f32[1024,512,3]{1,0,2:T(8,128)} %get-tuple-element.297, f32[3,512]{1,0:T(4,128)S(1)} %get-tuple-element.162, f32[3,512]{1,0:T(4,128)S(1)} %copy-done.106, f32[3,512]{1,0:T(4,128)S(1)} %copy-done.107, ...), kind=kLoop, calls=%fused_computation.14 | loop fusion | flops 33030144 | bytes 47765504 | tf_op jit(solution)/shard_map/while/body/eval_jaxpr/convert_element_type | solution.py:130
  222.7 1.7 fusion.118
  224.6 1.7 fusion.115
  226.5 1.7 fusion.112
  228.2 4.2 fusion.30
  232.4 4.6 %fusion.32 = (bf16[3,512,512]{1,2,0:T(8,128)(2,1)S(1)}, bf16[3,512,512]{1,2,0:T(8,128)(2,1)S(1)}, bf16[3,512,512]{1,2,0:T(8,128)(2,1)S(1)}) fusion(f32[512,512,3]{1,0,2:T(8,128)} %get-tuple-element.298, f32[3,512]{1,0:T(4,128)S(1)} %get-tuple-element.170, f32[3,512]{1,0:T(4,128)S(1)} %copy-done.100, f32[3,512]{1,0:T(4,128)S(1)} %copy-done.101, ...), kind=kLoop, calls=%fused_computation.66 | loop fusion | flops 16515072 | bytes 23910400 | tf_op jit(solution)/shard_map/while/body/eval_jaxpr/convert_element_type | solution.py:130
  248.1 1.2 convolution_convert_fusion.5
  249.4 1.2 fusion.164
  250.8 1.3 slice_bitcast_fusion.11
  252.8 3.2 fusion.42
  259.8 2.6 fusion.51
  262.7 3.6 concatenate.232
  266.4 4.2 concatenate.233
  271.7 6.0 %concatenate.234 = bf16[576,386]{0,1:T(8,128)(2,1)} concatenate(bf16[576,144]{0,1:T(8,128)(2,1)} %get-tuple-element.248, bf16[576,144]{0,1:T(8,128)(2,1)S(1)} %get-tuple-element.244, bf16[576,48]{0,1:T(8,128)(2,1)} %get-tuple-element.265, bf16[576,48]{0,1:T(8,128)(2,1)} %get-tuple-element.261, bf16[576,1]{0,1:T(2,128)(2,1)S(1)} %reshape.634, bf16[576,1]{0,1:T(2,128)(2,1)S(1)} %reshape.635), dimensions={1} | concatenate | bytes 889344 | tf_op jit(solution)/shard_map/concatenate | solution.py:161
  278.8 2.0 pad_maximum_fusion
  280.8 4.3 copy.350
  285.1 3.6 all-to-all-start
  288.8 2.5 slice_bitcast_fusion.9
  291.3 3.4 maximum_maximum_fusion
  294.7 22.5 %all-to-all-done = bf16[4,576,512]{2,1,0:T(8,128)(2,1)S(1)} async-done(((bf16[4,576,512]{2,1,0:T(8,128)(2,1)}), bf16[4,576,512]{2,1,0:T(8,128)(2,1)S(1)}, u32[]{:S(2)}, u32[]{:S(2)}) %all-to-all-start) | async-done | bytes 2359328 | tf_op jit(solution)/shard_map/all_to_all | solution.py:198
  317.2 5.0 %all-to-all-start.2 = ((bf16[4,576,1152]{2,1,0:T(8,128)(2,1)}), bf16[4,576,1152]{2,1,0:T(8,128)(2,1)}, u32[]{:S(2)}, u32[]{:S(2)}) async-start(bf16[4,576,1152]{2,1,0:T(8,128)(2,1)} %maximum_maximum_fusion), calls=%async_computation.2 | async-start | bytes 10616832 | tf_op jit(solution)/shard_map/all_to_all | solution.py:198
  322.3 1.3 reduce_sum.234
  323.6 58.8 %all-to-all-done.2 = bf16[4,576,1152]{2,1,0:T(8,128)(2,1)} async-done(((bf16[4,576,1152]{2,1,0:T(8,128)(2,1)}), bf16[4,576,1152]{2,1,0:T(8,128)(2,1)}, u32[]{:S(2)}, u32[]{:S(2)}) %all-to-all-start.2) | async-done | bytes 5308448 | tf_op jit(solution)/shard_map/all_to_all | solution.py:198
  382.4 5.5 %all-to-all-start.1 = ((bf16[8,72,512]{2,1,0:T(8,128)(2,1)}), bf16[8,72,512]{2,1,0:T(8,128)(2,1)}, u32[]{:S(2)}, u32[]{:S(2)}) async-start(bf16[8,72,512]{2,1,0:T(8,128)(2,1)} %bitcast.610), calls=%async_computation.1 | async-start | bytes 1179648 | tf_op jit(solution)/shard_map/all_to_all | solution.py:201
  387.9 4.8 %reduce_sum.236 = bf16[576,1152]{1,0:T(8,128)(2,1)} reduce(bf16[4,576,1152]{2,1,0:T(8,128)(2,1)} %all-to-all-done.2, bf16[]{:T(256)} %constant.83.clone.1), dimensions={0}, to_apply=%region_26.27 | reduce | flops 1990656 | bytes 6635522 | tf_op jit(solution)/shard_map/reduce_sum | solution.py:199
  392.8 10.9 %all-to-all-done.1 = bf16[8,72,512]{2,1,0:T(8,128)(2,1)} async-done(((bf16[8,72,512]{2,1,0:T(8,128)(2,1)}), bf16[8,72,512]{2,1,0:T(8,128)(2,1)}, u32[]{:S(2)}, u32[]{:S(2)}) %all-to-all-start.1) | async-done | bytes 589856 | tf_op jit(solution)/shard_map/all_to_all | solution.py:201
  403.6 4.3 all-to-all-start.3
  408.0 3.8 fusion.50
  412.6 3.0 add_convert_fusion
  420.4 18.9 %all-to-all-done.3 = bf16[8,72,1152]{2,1,0:T(8,128)(2,1)} async-done(((bf16[8,72,1152]{2,1,0:T(8,128)(2,1)}), bf16[8,72,1152]{2,1,0:T(8,128)(2,1)}, u32[]{:S(2)}, u32[]{:S(2)}) %all-to-all-start.3) | async-done | bytes 1327136 | tf_op jit(solution)/shard_map/all_to_all | solution.py:201
  439.2 1.5 convert_reduce_fusion
  (378 shorter events, 52.8 us)
Async XLA Ops:
  7.2 45.5 %copy-start.6 = (bf16[1024,576]{0,1:T(8,128)(2,1)S(1)}, bf16[1024,576]{0,1:T(8,128)(2,1)}, u32[]{:S(2)}) copy-start(bf16[1024,576]{0,1:T(8,128)(2,1)} %param.13) | copy-start | bytes 3538948
  7.2 45.8 %copy-start.110 = (s32[1,1024]{1,0:T(1,128)S(1)}, s32[1,1024]{1,0:T(1,128)}, u32[]{:S(2)}) copy-start(s32[1,1024]{1,0:T(1,128)} %param.14) | copy-start | bytes 12292
  7.2 51.2 %all-gather.6.cloned.1.call-start = ((), (), s32[]{:S(2)}) async-start(), calls=%async_computation.4 | async-start | bytes 1492992 | tf_op jit(solution)/shard_map/all_gather | solution.py:166
  8.9 74.2 %all-gather.8.cloned.1.call-start = ((), (), s32[]{:S(2)}) async-start(), calls=%async_computation.5 | async-start | bytes 2949120 | tf_op jit(solution)/shard_map/all_gather | solution.py:167
  50.8 74.6 %all-gather.10.cloned.1.call-start = ((), (), s32[]{:S(2)}) async-start(), calls=%async_computation.6 | async-start | bytes 6635520 | tf_op jit(solution)/shard_map/all_gather | solution.py:167
  52.7 38.5 %copy-start.14 = (f32[1024,64]{0,1:T(8,128)}, f32[1024,64]{0,1:T(8,128)S(1)}, u32[]{:S(2)}) copy-start(f32[1024,64]{0,1:T(8,128)S(1)} %get-tuple-element.273) | copy-start | bytes 786436
  52.7 38.8 %copy-start.12 = (f32[1024,64]{0,1:T(8,128)}, f32[1024,64]{0,1:T(8,128)S(1)}, u32[]{:S(2)}) copy-start(f32[1024,64]{0,1:T(8,128)S(1)} %get-tuple-element.272) | copy-start | bytes 786436
  53.0 52.5 %copy-start.97 = (f32[1024]{0:T(1024)}, f32[1024]{0:T(1024)S(1)}, u32[]{:S(2)}) copy-start(f32[1024]{0:T(1024)S(1)} %add_rsqrt_fusion.1) | copy-start | bytes 12292
  53.2 55.5 %copy-start.24 = (pred[512,512]{0,1:T(8,128)(4,1)}, pred[512,512]{0,1:T(8,128)(4,1)S(1)}, u32[]{:S(2)}) copy-start(pred[512,512]{0,1:T(8,128)(4,1)S(1)} %fusion.121) | copy-start | bytes 786436
  53.7 60.3 %copy-start.18 = (pred[512,1024]{0,1:T(8,128)(4,1)}, pred[512,1024]{0,1:T(8,128)(4,1)S(1)}, u32[]{:S(2)}) copy-start(pred[512,1024]{0,1:T(8,128)(4,1)S(1)} %fusion.57) | copy-start | bytes 1572868
  84.5 21.1 %copy-start.95 = (f32[576]{0:T(1024)}, f32[576]{0:T(1024)S(1)}, u32[]{:S(2)}) copy-start(f32[576]{0:T(1024)S(1)} %get-tuple-element.161) | copy-start | bytes 6916
  86.3 19.3 %copy-start.54 = (bf16[576,48]{1,0:T(8,128)(2,1)}, bf16[576,48]{1,0:T(8,128)(2,1)S(1)}, u32[]{:S(2)}) copy-start(bf16[576,48]{1,0:T(8,128)(2,1)S(1)} %get-tuple-element.197) | copy-start | bytes 165892
  86.3 19.3 %copy-start.56 = (bf16[576,48]{1,0:T(8,128)(2,1)}, bf16[576,48]{1,0:T(8,128)(2,1)S(1)}, u32[]{:S(2)}) copy-start(bf16[576,48]{1,0:T(8,128)(2,1)S(1)} %get-tuple-element.202) | copy-start | bytes 165892
  86.3 19.3 %copy-start.58 = (bf16[576,48]{1,0:T(8,128)(2,1)}, bf16[576,48]{1,0:T(8,128)(2,1)S(1)}, u32[]{:S(2)}) copy-start(bf16[576,48]{1,0:T(8,128)(2,1)S(1)} %get-tuple-element.203) | copy-start | bytes 165892
  86.3 19.3 %copy-start.60 = (bf16[576,48]{1,0:T(8,128)(2,1)}, bf16[576,48]{1,0:T(8,128)(2,1)S(1)}, u32[]{:S(2)}) copy-start(bf16[576,48]{1,0:T(8,128)(2,1)S(1)} %get-tuple-element.204) | copy-start | bytes 165892
  91.2 8.3 %copy-start.20 = (bf16[1024,192]{0,1:T(8,128)(2,1)}, bf16[1024,192]{0,1:T(8,128)(2,1)S(1)}, u32[]{:S(2)}) copy-start(bf16[1024,192]{0,1:T(8,128)(2,1)S(1)} %fusion.123) | copy-start | bytes 1179652
  92.3 3.7 copy-start.37
  92.3 7.2 %copy-start.39 = (bf16[512,192]{0,1:T(8,128)(2,1)}, bf16[512,192]{0,1:T(8,128)(2,1)S(1)}, u32[]{:S(2)}) copy-start(bf16[512,192]{0,1:T(8,128)(2,1)S(1)} %get-tuple-element.235) | copy-start | bytes 589828
  92.9 14.8 %copy-start.1 = (f32[512,512,3]{1,0,2:T(8,128)}, f32[512,512,3]{1,0,2:T(8,128)S(1)}, u32[]{:S(2)}) copy-start(f32[512,512,3]{1,0,2:T(8,128)S(1)} %fusion.145) | copy-start | bytes 9437188
  93.9 18.0 %copy-start = (f32[1024,512,3]{1,0,2:T(8,128)}, f32[1024,512,3]{1,0,2:T(8,128)S(1)}, u32[]{:S(2)}) copy-start(f32[1024,512,3]{1,0,2:T(8,128)S(1)} %fusion.139) | copy-start | bytes 18874372
  94.7 14.1 %copy-start.22 = (f32[512,512,3]{1,0,2:T(8,128)}, f32[512,512,3]{1,0,2:T(8,128)S(1)}, u32[]{:S(2)}) copy-start(f32[512,512,3]{1,0,2:T(8,128)S(1)} %get-tuple-element.292) | copy-start | bytes 9437188
  96.0 18.0 %copy-start.16 = (f32[1024,512,3]{1,0,2:T(8,128)}, f32[1024,512,3]{1,0,2:T(8,128)S(1)}, u32[]{:S(2)}) copy-start(f32[1024,512,3]{1,0,2:T(8,128)S(1)} %get-tuple-element.289) | copy-start | bytes 18874372
  97.8 8.7 %copy-start.4 = (f32[512,512,3]{1,0,2:T(8,128)}, f32[512,512,3]{1,0,2:T(8,128)S(1)}, u32[]{:S(2)}) copy-start(f32[512,512,3]{1,0,2:T(8,128)S(1)} %get-tuple-element.293) | copy-start | bytes 9437188
  102.8 7.1 %copy-start.3 = (f32[1024,512,3]{1,0,2:T(8,128)}, f32[1024,512,3]{1,0,2:T(8,128)S(1)}, u32[]{:S(2)}) copy-start(f32[1024,512,3]{1,0,2:T(8,128)S(1)} %get-tuple-element.290) | copy-start | bytes 18874372
  106.6 7.5 %copy-start.70 = (bf16[1024,192]{0,1:T(8,128)(2,1)}, bf16[1024,192]{0,1:T(8,128)(2,1)S(1)}, u32[]{:S(2)}) copy-start(bf16[1024,192]{0,1:T(8,128)(2,1)S(1)} %convolution_convert_fusion.6) | copy-start | bytes 1179652
  107.7 8.5 %copy-start.115 = (bf16[64,3,512]{2,0,1:T(8,128)(2,1)}, bf16[64,3,512]{2,0,1:T(8,128)(2,1)S(1)}, u32[]{:S(2)}) copy-start(bf16[64,3,512]{2,0,1:T(8,128)(2,1)S(1)} %fusion.71) | copy-start | bytes 589828
  108.8 7.4 %copy-start.117 = (bf16[64,3,512]{2,0,1:T(8,128)(2,1)}, bf16[64,3,512]{2,0,1:T(8,128)(2,1)S(1)}, u32[]{:S(2)}) copy-start(bf16[64,3,512]{2,0,1:T(8,128)(2,1)S(1)} %fusion.70) | copy-start | bytes 589828
  109.9 6.3 %copy-start.119 = (bf16[64,3,512]{2,0,1:T(8,128)(2,1)}, bf16[64,3,512]{2,0,1:T(8,128)(2,1)S(1)}, u32[]{:S(2)}) copy-start(bf16[64,3,512]{2,0,1:T(8,128)(2,1)S(1)} %fusion.72) | copy-start | bytes 589828
  112.0 4.2 copy-start.121
  117.5 54.6 %copy-start.8 = (f32[1024,576]{0,1:T(8,128)}, f32[1024,576]{0,1:T(8,128)S(1)}, u32[]{:S(2)}) copy-start(f32[1024,576]{0,1:T(8,128)S(1)} %get-tuple-element.295) | copy-start | bytes 7077892
  128.5 20.4 %copy-start.62 = (bf16[576,384]{1,0:T(8,128)(2,1)}, bf16[576,384]{1,0:T(8,128)(2,1)S(1)}, u32[]{:S(2)}) copy-start(bf16[576,384]{1,0:T(8,128)(2,1)S(1)} %get-tuple-element.183) | copy-start | bytes 1327108
  128.5 20.4 %copy-start.64 = (bf16[576,384]{1,0:T(8,128)(2,1)}, bf16[576,384]{1,0:T(8,128)(2,1)S(1)}, u32[]{:S(2)}) copy-start(bf16[576,384]{1,0:T(8,128)(2,1)S(1)} %get-tuple-element.184) | copy-start | bytes 1327108
  128.5 20.4 %copy-start.66 = (bf16[576,384]{1,0:T(8,128)(2,1)}, bf16[576,384]{1,0:T(8,128)(2,1)S(1)}, u32[]{:S(2)}) copy-start(bf16[576,384]{1,0:T(8,128)(2,1)S(1)} %get-tuple-element.185) | copy-start | bytes 1327108
  128.6 20.4 %copy-start.68 = (bf16[576,384]{1,0:T(8,128)(2,1)}, bf16[576,384]{1,0:T(8,128)(2,1)S(1)}, u32[]{:S(2)}) copy-start(bf16[576,384]{1,0:T(8,128)(2,1)S(1)} %get-tuple-element.186) | copy-start | bytes 1327108
  143.9 5.0 %copy-start.35 = (bf16[1024,576]{0,1:T(8,128)(2,1)S(1)}, bf16[1024,576]{0,1:T(8,128)(2,1)}, u32[]{:S(2)}) copy-start(bf16[1024,576]{0,1:T(8,128)(2,1)} %param.25) | copy-start | bytes 3538948
  158.5 4.1 copy-start.129
  175.5 9.5 %slice-start = ((s8[6291456]{0:T(1024)(128)(4,1)}), s8[4194304]{0:T(1024)(128)(4,1)S(1)}, s32[]{:S(2)}) async-start(s8[6291456]{0:T(1024)(128)(4,1)} %bitcast.583), calls=%async_computation.7 | async-start | bytes 8388608
  177.7 7.3 %slice-start.1 = ((s8[6291456]{0:T(1024)(128)(4,1)}), s8[2097152]{0:T(1024)(128)(4,1)S(1)}, s32[]{:S(2)}) async-start(s8[6291456]{0:T(1024)(128)(4,1)} %bitcast.583), calls=%async_computation.8 | async-start | bytes 4194304
  181.4 3.7 copy-start.19
  181.4 3.7 copy-start.104
  181.4 3.7 copy-start.109
  181.4 6.5 %slice-start.2 = ((s8[6291456]{0:T(1024)(128)(4,1)}), s8[4194304]{0:T(1024)(128)(4,1)S(1)}, s32[]{:S(2)}) async-start(s8[6291456]{0:T(1024)(128)(4,1)} %bitcast.585), calls=%async_computation.9 | async-start | bytes 8388608
  185.1 6.0 %slice-start.4 = ((s8[6291456]{0:T(1024)(128)(4,1)}), s8[4194304]{0:T(1024)(128)(4,1)S(1)}, s32[]{:S(2)}) async-start(s8[6291456]{0:T(1024)(128)(4,1)} %bitcast.589), calls=%async_computation.11 | async-start | bytes 8388608
  187.9 3.2 slice-start.5
  205.1 12.3 %copy-start.44 = (bf16[512,192]{0,1:T(8,128)(2,1)S(1)}, bf16[512,192]{0,1:T(8,128)(2,1)}, u32[]{:S(2)}) copy-start(bf16[512,192]{0,1:T(8,128)(2,1)} %copy-done.43) | copy-start | bytes 589828
  232.4 5.0 %copy-start.42 = (bf16[512,192]{0,1:T(8,128)(2,1)S(1)}, bf16[512,192]{0,1:T(8,128)(2,1)}, u32[]{:S(2)}) copy-start(bf16[512,192]{0,1:T(8,128)(2,1)} %copy-done.41) | copy-start | bytes 589828
  249.4 3.4 copy-start.127
  252.8 4.0 copy-start.88
  252.8 4.0 copy-start.89
  252.8 4.0 copy-start.92
  252.8 4.0 copy-start.93
  252.8 4.0 copy-start.94
  262.4 4.0 copy-start.90
  285.1 32.1 %all-to-all-start = ((bf16[4,576,512]{2,1,0:T(8,128)(2,1)}), bf16[4,576,512]{2,1,0:T(8,128)(2,1)S(1)}, u32[]{:S(2)}, u32[]{:S(2)}) async-start(bf16[4,576,512]{2,1,0:T(8,128)(2,1)} %copy.350), calls=%async_computation | async-start | bytes 4718592 | tf_op jit(solution)/shard_map/all_to_all | solution.py:198
  317.2 65.2 %all-to-all-start.2 = ((bf16[4,576,1152]{2,1,0:T(8,128)(2,1)}), bf16[4,576,1152]{2,1,0:T(8,128)(2,1)}, u32[]{:S(2)}, u32[]{:S(2)}) async-start(bf16[4,576,1152]{2,1,0:T(8,128)(2,1)} %maximum_maximum_fusion), calls=%async_computation.2 | async-start | bytes 10616832 | tf_op jit(solution)/shard_map/all_to_all | solution.py:198
  382.4 21.2 %all-to-all-start.1 = ((bf16[8,72,512]{2,1,0:T(8,128)(2,1)}), bf16[8,72,512]{2,1,0:T(8,128)(2,1)}, u32[]{:S(2)}, u32[]{:S(2)}) async-start(bf16[8,72,512]{2,1,0:T(8,128)(2,1)} %bitcast.610), calls=%async_computation.1 | async-start | bytes 1179648 | tf_op jit(solution)/shard_map/all_to_all | solution.py:201
  387.9 20.0 %copy-start.11 = (f32[1024,576]{0,1:T(8,128)S(1)}, f32[1024,576]{0,1:T(8,128)}, u32[]{:S(2)}) copy-start(f32[1024,576]{0,1:T(8,128)} %copy-done.10) | copy-start | bytes 7077892
  403.6 35.6 %all-to-all-start.3 = ((bf16[8,72,1152]{2,1,0:T(8,128)(2,1)}), bf16[8,72,1152]{2,1,0:T(8,128)(2,1)}, u32[]{:S(2)}, u32[]{:S(2)}) async-start(bf16[8,72,1152]{2,1,0:T(8,128)(2,1)} %bitcast.595), calls=%async_computation.3 | async-start | bytes 2654208 | tf_op jit(solution)/shard_map/all_to_all | solution.py:201
  407.9 3.9 copy-start.9
  407.9 3.8 copy-start.63
  407.9 3.8 copy-start.65
  408.0 3.8 copy-start.67
  408.0 3.8 copy-start.69
  408.0 4.7 %copy-start.128 = (bf16[1024,1536]{1,0:T(8,128)(2,1)S(1)}, bf16[1024,1536]{1,0:T(8,128)(2,1)}, u32[]{:S(2)}) copy-start(bf16[1024,1536]{1,0:T(8,128)(2,1)} %get-tuple-element.182) | copy-start | bytes 9437188
  (79 other events, 154.3 us)
Sparse Core Ops, SparseCore 0:
  10.8 47.5 all-gather.5
  59.9 23.0 all-gather.7
  84.6 40.7 all-gather.9

commit v2 on v1

--- a/solution.py
+++ b/solution.py
@@ -185,7 +185,7 @@
     ]
 
 
-def reduce_pack(matrices, vectors, model_part):
+def pack_grads(matrices, vectors=()):
     pieces = lax.axis_size("dp")
     blocks = []
     for piece in range(pieces):
@@ -194,8 +194,14 @@
             width = matrix.shape[1] // pieces
             columns.append(matrix[:, piece * width : (piece + 1) * width])
         blocks.append(pack_columns(columns + list(vectors)).astype(jnp.bfloat16))
-    sent = jnp.stack(blocks)
-    got = lax.all_to_all(sent, "dp", 0, 0, tiled=True)
+    return jnp.stack(blocks)
+
+
+def exchange(sent):
+    return lax.all_to_all(sent, "dp", 0, 0, tiled=True)
+
+
+def reduce_pack(got, model_part):
     half = jnp.sum(got.astype(jnp.float32), axis=0)
     shares = half.reshape(half.shape[0] // model_part, model_part, half.shape[1])
     shares = lax.all_to_all(shares.astype(jnp.bfloat16), "fsdp", 0, 0, tiled=True)
@@ -225,6 +231,7 @@
     )
     mlp_pack = pack_columns((w_gate, w_up, w_down.T))
     attn_all = gather_pack(attn_pack)
+    mlp_pack, attn_all = lax.optimization_barrier((mlp_pack, attn_all))
     mlp_all = gather_pack(mlp_pack)
     full_query, full_output, full_key, full_value, gains_attn, gains_mlp = split_full(
         attn_all, attn_widths
@@ -301,6 +308,9 @@
     grad_resid = cotangent.astype(jnp.float32) + norm_back(
         grad_normed_mlp * back_weights[1].astype(jnp.float32), scaled_mlp, inverse_mlp
     )
+    mlp_sent = pack_grads((grad_gate, grad_up, grad_down))
+    grad_resid, mlp_sent = lax.optimization_barrier((grad_resid, mlp_sent))
+    mlp_got = exchange(mlp_sent)
     grad_branch = grad_resid.astype(jnp.bfloat16)
     grad_output = jnp.einsum("rd,rq->dq", grad_branch, mixture, preferred_element_type=jnp.float32)
     grad_mixture = jnp.einsum(
@@ -329,6 +339,8 @@
         .astype(jnp.bfloat16)
     )
     grad_value_raw = grad_values.reshape(row_count, KVW).astype(jnp.bfloat16)
+    grad_query_raw, mlp_got = lax.optimization_barrier((grad_query_raw, mlp_got))
+    mlp_sum = reduce_pack(mlp_got, model_part)
     grad_query = jnp.einsum(
         "rd,rq->dq", normed_attn, grad_query_raw, preferred_element_type=jnp.float32
     )
@@ -351,12 +363,11 @@
     grad_tokens = grad_resid + norm_back(
         grad_normed_attn * back_weights[0].astype(jnp.float32), scaled_attn, inverse_attn
     )
-    mlp_sum = reduce_pack((grad_gate, grad_up, grad_down), (), model_part)
-    attn_sum = reduce_pack(
+    attn_sent = pack_grads(
         (grad_query, grad_output, grad_key, grad_value),
         (grad_attn_gain[:, None], grad_mlp_gain[:, None]),
-        model_part,
-    )
+    )
+    attn_sum = reduce_pack(exchange(attn_sent), model_part)
     own_gate, own_up, own_down = split_columns(mlp_sum, mlp_widths)
     own_query, own_output, own_key, own_value, own_attn_gain, own_mlp_gain = split_columns(
         attn_sum, attn_widths

time: 453 us -> 479 us (1.057)
  waiting for transfers between devices: 147 us -> 159 us
  other arithmetic: 49.4 us -> 57.8 us
  local copies, waits for them, and re-layouts: 52.7 us -> 60.4 us
    all_gather x1, waiting for transfers between devices: 4.64 us -> 21.5 us  [gather_pack(): rows = lax.all_gather(packed, 'fsdp', axis=0, tiled=True)]
    all_to_all x2, waiting for transfers between devices: 81.3 us -> 66.8 us  [exchange(): return lax.all_to_all(sent, 'dp', 0, 0, tiled=True)]
    dot_general x1, matrix products: 15.3 us -> 2.86 us  [on_device(): up_pre = jnp.dot(normed_mlp, weights[7], preferred_element_type=jnp.float32)]
    all_gather x2, waiting for transfers between devices: 31 us -> 37 us  [gather_pack(): return lax.all_gather(rows, 'dp', axis=0, tiled=False)]
    unnamed x278 -> x388, local copies, waits for them, and re-layouts: 10.8 us -> 16 us
  transfers between devices with their start and end apart: 7 -> 7, of which waited for: 7 -> 7; matrix products, arithmetic and copies ran while one was open for 15% -> 16% of each run, Pallas kernels for 0% -> 0%
where the time goes in v2:
time: 479 us; the launch traced here: 474 us
  waiting for transfers between devices  159 us (33%)
  matrix products  127 us (27%)
  local copies, waits for them, and re-layouts  60.4 us (13%)
  other arithmetic  57.8 us (12%)
  blocking collectives  35.4 us (7%)
  starting transfers between devices  18.6 us (4%)
  between operations  16.6 us (3%)
    all_to_all x2, waiting for transfers between devices, exchange(): return lax.all_to_all(sent, 'dp', 0, 0, tiled=True)  66.8 us
    all_gather x2, waiting for transfers between devices, gather_pack(): return lax.all_gather(rows, 'dp', axis=0, tiled=False)  37 us
    all_gather x1, blocking collectives, gather_pack(): rows = lax.all_gather(packed, 'fsdp', axis=0, tiled=True)  35.4 us
    all_to_all x2, waiting for transfers between devices, reduce_pack(): lax.all_to_all(shares.astype(jnp.bfloat16), 'fsdp', 0, 0, tiled=True)  33.5 us
    dot_general x6, matrix products, attend_backward(): jnp.einsum('qgd,td->gqt', grad_block, value_head, preferred_element_type=...  24 us
    all_gather x1, waiting for transfers between devices, gather_pack(): rows = lax.all_gather(packed, 'fsdp', axis=0, tiled=True)  21.5 us
    concatenate x7, local copies, waits for them, and re-layouts, pack_columns(): packed = jnp.concatenate(parts, axis=-1)  18.9 us
    convert_element_type x2, other arithmetic, attend_backward(): grad_scores = (prob_full * (grad_probs - delta)).astype(jnp.bfloat16)  17.1 us
  transfers between devices with their start and end apart: 7, of which 7 were waited for; matrix products, arithmetic and copies ran while one was open for 16% of the time, Pallas kernels for 0%

profile of v2, /device:TPU:0, one launch (start us, length us, event | category | flops | bytes accessed | tf_op | source)
XLA Modules:
  0.0 474.5 jit_solution(9306203340219172050)
XLA Ops:
  12.3 35.4 %all_gather.18 = bf16[576,512]{1,0:T(8,128)(2,1)} all-gather(bf16[72,512]{1,0:T(8,128)(2,1)S(1)} %pad.21), channel_id=1, replica_groups=mesh['dp'=4,'fsdp'=8] {'fsdp'}, dimensions={0}, use_global_device_ids=true | all-gather | bytes 663552 | tf_op jit(solution)/shard_map/all_gather | solution.py:166
  51.4 21.5 %all-gather.8.cloned.1.call-done = bf16[2304,512]{1,0:T(8,128)(2,1)} async-done(((bf16[576,512]{1,0:T(8,128)(2,1)}), bf16[2304,512]{1,0:T(8,128)(2,1)}) %all-gather.8.cloned.1.call-update) | async-done | bytes 2359312 | tf_op jit(solution)/shard_map/all_gather | solution.py:167
  72.9 2.0 convert_reduce_fusion.2
  74.9 2.5 slice_bitcast_fusion.39
  77.4 1.9 slice_bitcast_fusion.31
  80.9 1.6 fusion.165
  86.0 1.3 fusion.17
  88.8 2.8 fusion.43
  91.6 1.9 fusion.44
  93.6 6.4 %fusion.14 = (f32[3,512]{1,0:T(4,128)}, f32[3,512]{1,0:T(4,128)}, f32[3,512]{1,0:T(4,128)}, f32[1024,512,3]{1,0,2:T(8,128)}) fusion(f32[1024,512,3]{1,0,2:T(8,128)S(1)} %get-tuple-element.301, f32[3,512]{1,0:T(4,128)S(1)} %get-tuple-element.300, pred[512,1024]{0,1:T(8,128)(4,1)S(1)} %copy-done.20, f32[1024,512,3]{1,0,2:T(8,128)S(1)} %fusion.139, ...), kind=kOutput, calls=%fused_computation.36 | convolution fusion | flops 217050624 | bytes 19752960 | tf_op jit(solution)/shard_map/while/body/eval_jaxpr/qgd,td->gqt/dot_general | solution.py:64
  100.0 21.5 %all-gather.6.cloned.1.call-done = bf16[576,1152]{1,0:T(8,128)(2,1)} async-done(((bf16[72,1152]{1,0:T(8,128)(2,1)}), bf16[576,1152]{1,0:T(8,128)(2,1)}) %all-gather.6.cloned.1.call-update) | async-done | bytes 1327120 | tf_op jit(solution)/shard_map/all_gather | solution.py:166
  123.0 6.4 %fusion.15 = (f32[3,512]{1,0:T(4,128)S(1)}, f32[3,512]{1,0:T(4,128)S(1)}) fusion(f32[1024,512,3]{1,0,2:T(8,128)} %get-tuple-element.302, f32[3,512]{1,0:T(4,128)} %get-tuple-element.178, pred[512,1024]{0,1:T(8,128)(4,1)} %copy-done.19, f32[3,512]{1,0:T(4,128)} %get-tuple-element.179, f32[1024,512,3]{1,0,2:T(8,128)} %copy-done), kind=kLoop, calls=%fused_computation.37 | loop fusion | flops 12579840 | bytes 13131776 | tf_op jit(solution)/shard_map/while/body/eval_jaxpr/reduce_sum | solution.py:82
  136.9 2.0 fusion.74
  139.0 2.0 fusion.73
  141.1 2.0 fusion.75
  145.8 1.3 multiply_convert_fusion.1
  147.1 15.5 %all-gather.10.cloned.1.call-done = bf16[2304,1152]{1,0:T(8,128)(2,1)} async-done(((bf16[576,1152]{1,0:T(8,128)(2,1)}), bf16[2304,1152]{1,0:T(8,128)(2,1)}) %all-gather.10.cloned.1.call-update) | async-done | bytes 5308432 | tf_op jit(solution)/shard_map/all_gather | solution.py:167
  162.6 3.2 slice_bitcast_fusion.15
  165.9 2.9 fusion.129
  168.8 5.0 %fusion.131 = f32[1024,1536]{1,0:T(8,128)} fusion(bf16[1024,576]{0,1:T(8,128)(2,1)S(1)} %copy-done.43, bf16[576,384]{1,0:T(8,128)(2,1)S(1)} %get-tuple-element.203, bf16[576,384]{1,0:T(8,128)(2,1)S(1)} %get-tuple-element.204, bf16[576,384]{1,0:T(8,128)(2,1)S(1)} %get-tuple-element.205, bf16[576,384]{1,0:T(8,128)(2,1)S(1)} %get-tuple-element.206), kind=kOutput, calls=%fused_computation.236 | convolution fusion | flops 1819017216 | bytes 9240576 | tf_op jit(solution)/shard_map/dot_general | solution.py:281
  173.8 9.6 %fusion.12 = (bf16[1024,1536]{1,0:T(8,128)(2,1)S(1)}, bf16[1024,1536]{1,0:T(8,128)(2,1)}, bf16[1024,1536]{1,0:T(8,128)(2,1)}) fusion(f32[1024,1536]{1,0:T(8,128)} %fusion.131, f32[1024,1536]{1,0:T(8,128)S(1)} %fusion.129, bf16[1024,576]{0,1:T(8,128)(2,1)S(1)} %copy-done.42, bf16[576,384]{1,0:T(8,128)(2,1)S(1)} %get-tuple-element.196, ...), kind=kOutput, calls=%fused_computation.20 | convolution fusion | flops 1842610176 | bytes 24969216 | tf_op jit(solution)/shard_map/rd,df->rf/dot_general | solution.py:289
  183.3 5.1 %fusion.130 = f32[1024,576]{0,1:T(8,128)S(1)} fusion(bf16[1024,1536]{1,0:T(8,128)(2,1)} %get-tuple-element.193, bf16[576,384]{1,0:T(8,128)(2,1)S(1)} %get-tuple-element.203, bf16[576,384]{1,0:T(8,128)(2,1)S(1)} %get-tuple-element.204, bf16[576,384]{1,0:T(8,128)(2,1)S(1)} %get-tuple-element.205, bf16[576,384]{1,0:T(8,128)(2,1)S(1)} %get-tuple-element.206), kind=kOutput, calls=%fused_computation.235 | convolution fusion | flops 1819017216 | bytes 7274496 | tf_op jit(solution)/shard_map/rf,df->rd/dot_general | solution.py:301
  188.5 2.0 convolution_convert_fusion.2
  190.5 2.0 convolution_convert_fusion.1
  192.5 5.0 %multiply_reduce_fusion = (bf16[576]{0:T(1024)(128)(2,1)}, f32[1024]{0:T(1024)S(1)}, f32[1024,576]{0,1:T(8,128)S(1)}) fusion(f32[1024,576]{0,1:T(8,128)S(1)} %get-tuple-element.307, f32[1024]{0:T(1024)S(1)} %add_rsqrt_fusion, f32[576]{0:T(1024)S(1)} %copy-done.123, f32[1024,576]{0,1:T(8,128)S(1)} %fusion.130, bf16[1024,1536]{1,0:T(8,128)(2,1)} %copy-done.176, ...), kind=kOutput, calls=%fused_computation.111 | convolution fusion | flops 1823144448 | bytes 12004736 | tf_op jit(solution)/shard_map/rf,df->rd/dot_general | solution.py:304
  197.6 1.7 copy-done.177
  199.3 2.0 fusion.42
  202.5 3.6 maximum_maximum_fusion
  206.2 1.5 convolution_convert_fusion.3
  208.4 3.7 fusion.136
  212.1 3.6 fusion.138
  215.8 2.8 fusion.82
  218.6 2.8 fusion.79
  221.4 2.8 fusion.76
  224.2 11.2 %fusion.6 = (f32[3,512]{1,0:T(4,128)S(1)}, f32[3,512]{1,0:T(4,128)S(1)}, f32[3,512]{1,0:T(4,128)S(1)}, f32[1024,512,3]{1,0,2:T(8,128)}) fusion(f32[3,512]{1,0:T(4,128)S(1)} %copy-done.141, f32[3,512]{1,0:T(4,128)S(1)} %copy-done.142, f32[1024,512,3]{1,0,2:T(8,128)} %copy-done.17, pred[512,1024]{0,1:T(8,128)(4,1)S(1)} %copy-done.21, ...), kind=kOutput, calls=%fused_computation.12 | convolution fusion | flops 229633536 | bytes 38668288 | tf_op jit(solution)/shard_map/while/body/eval_jaxpr/qgd,td->gqt/dot_general | solution.py:120
  235.3 12.7 %fusion.8 = (bf16[3,512,1024]{1,2,0:T(8,128)(2,1)S(1)}, bf16[3,512,1024]{1,2,0:T(8,128)(2,1)S(1)}, bf16[3,512,1024]{1,2,0:T(8,128)(2,1)S(1)}) fusion(f32[1024,512,3]{1,0,2:T(8,128)} %get-tuple-element.309, f32[3,512]{1,0:T(4,128)S(1)} %get-tuple-element.174, f32[3,512]{1,0:T(4,128)S(1)} %copy-done.141, f32[3,512]{1,0:T(4,128)S(1)} %copy-done.142, ...), kind=kLoop, calls=%fused_computation.14 | loop fusion | flops 33030144 | bytes 47765504 | tf_op jit(solution)/shard_map/while/body/eval_jaxpr/convert_element_type | solution.py:130
  249.1 1.4 convolution_multiply_fusion.2
  253.6 4.3 fusion.30
  257.9 4.4 fusion.32
  265.9 1.5 convolution_multiply_fusion.1
  270.5 1.4 convolution_multiply_fusion
  276.0 5.4 %all-to-all-start = ((bf16[4,576,1152]{2,1,0:T(8,128)(2,1)}), bf16[4,576,1152]{2,1,0:T(8,128)(2,1)}, u32[]{:S(2)}, u32[]{:S(2)}) async-start(bf16[4,576,1152]{2,1,0:T(8,128)(2,1)} %maximum_maximum_fusion), calls=%async_computation | async-start | bytes 10616832 | tf_op jit(solution)/shard_map/all_to_all | solution.py:201
  281.4 1.4 maximum_maximum_fusion.3
  285.6 1.6 fusion.56
  298.4 43.1 %all-to-all-done = bf16[4,576,1152]{2,1,0:T(8,128)(2,1)} async-done(((bf16[4,576,1152]{2,1,0:T(8,128)(2,1)}), bf16[4,576,1152]{2,1,0:T(8,128)(2,1)}, u32[]{:S(2)}, u32[]{:S(2)}) %all-to-all-start) | async-done | bytes 5308448 | tf_op jit(solution)/shard_map/all_to_all | solution.py:201
  341.5 2.6 convolution_convert_fusion.5
  346.4 2.6 fusion.51
  349.0 3.7 concatenate.247
  352.7 3.6 concatenate.248
  356.5 4.2 concatenate.249
  361.8 5.8 %concatenate.250 = bf16[576,386]{0,1:T(8,128)(2,1)} concatenate(bf16[576,144]{0,1:T(8,128)(2,1)} %get-tuple-element.260, bf16[576,144]{0,1:T(8,128)(2,1)S(1)} %copy-done.62, bf16[576,48]{0,1:T(8,128)(2,1)} %get-tuple-element.277, bf16[576,48]{0,1:T(8,128)(2,1)} %get-tuple-element.273, bf16[576,1]{0,1:T(2,128)(2,1)S(1)} %reshape.634, bf16[576,1]{0,1:T(2,128)(2,1)S(1)} %reshape.635), dimensions={1} | concatenate | bytes 889344 | tf_op jit(solution)/shard_map/concatenate | solution.py:161
  368.7 2.1 pad_maximum_fusion
  370.8 4.5 copy.350
  375.3 3.6 all-to-all-start.1
  378.9 4.7 reduce_sum.236
  383.6 23.7 %all-to-all-done.1 = bf16[4,576,512]{2,1,0:T(8,128)(2,1)S(1)} async-done(((bf16[4,576,512]{2,1,0:T(8,128)(2,1)}), bf16[4,576,512]{2,1,0:T(8,128)(2,1)S(1)}, u32[]{:S(2)}, u32[]{:S(2)}) %all-to-all-start.1) | async-done | bytes 2359328 | tf_op jit(solution)/shard_map/all_to_all | solution.py:201
  407.3 5.5 %all-to-all-start.3 = ((bf16[8,72,1152]{2,1,0:T(8,128)(2,1)}), bf16[8,72,1152]{2,1,0:T(8,128)(2,1)}, u32[]{:S(2)}, u32[]{:S(2)}) async-start(bf16[8,72,1152]{2,1,0:T(8,128)(2,1)} %bitcast.601), calls=%async_computation.3 | async-start | bytes 2654208 | tf_op jit(solution)/shard_map/all_to_all | solution.py:207
  412.9 6.2 %add_convert_fusion = bf16[1024,576]{0,1:T(8,128)(2,1)} fusion(f32[1024,576]{0,1:T(8,128)} %copy-done.10, bf16[1024,1536]{1,0:T(8,128)(2,1)} %get-tuple-element.194, bf16[576,384]{1,0:T(8,128)(2,1)} %copy-done.81, bf16[576,384]{1,0:T(8,128)(2,1)} %copy-done.82, bf16[576,384]{1,0:T(8,128)(2,1)} %copy-done.83, bf16[576,384]{1,0:T(8,128)(2,1)} %copy-done.80), kind=kOutput, calls=%fused_computation.115 | convolution fusion | flops 1820196864 | bytes 8454144 | tf_op jit(solution)/shard_map/rf,df->rd/dot_general | solution.py:284
  419.1 1.3 reduce_sum.234
  420.4 24.0 %all-to-all-done.3 = bf16[8,72,1152]{2,1,0:T(8,128)(2,1)} async-done(((bf16[8,72,1152]{2,1,0:T(8,128)(2,1)}), bf16[8,72,1152]{2,1,0:T(8,128)(2,1)}, u32[]{:S(2)}, u32[]{:S(2)}) %all-to-all-start.3) | async-done | bytes 1327136 | tf_op jit(solution)/shard_map/all_to_all | solution.py:207
  444.4 3.6 all-to-all-start.2
  448.0 4.4 fusion.50
  452.4 1.5 convert_reduce_fusion
  454.7 9.4 %all-to-all-done.2 = bf16[8,72,512]{2,1,0:T(8,128)(2,1)S(1)} async-done(((bf16[8,72,512]{2,1,0:T(8,128)(2,1)}), bf16[8,72,512]{2,1,0:T(8,128)(2,1)S(1)}, u32[]{:S(2)}, u32[]{:S(2)}) %all-to-all-start.2) | async-done | bytes 589856 | tf_op jit(solution)/shard_map/all_to_all | solution.py:207
  (491 shorter events, 65.4 us)
Async XLA Ops:
  7.2 42.4 %copy-start.7 = (bf16[1024,576]{0,1:T(8,128)(2,1)S(1)}, bf16[1024,576]{0,1:T(8,128)(2,1)}, u32[]{:S(2)}) copy-start(bf16[1024,576]{0,1:T(8,128)(2,1)} %param.13) | copy-start | bytes 3538948
  7.2 42.7 %copy-start.153 = (s32[1,1024]{1,0:T(1,128)S(1)}, s32[1,1024]{1,0:T(1,128)}, u32[]{:S(2)}) copy-start(s32[1,1024]{1,0:T(1,128)} %param.14) | copy-start | bytes 12292
  7.2 42.9 %copy-start.117 = (bf16[384,72]{0,1:T(8,128)(2,1)S(1)}, bf16[384,72]{0,1:T(8,128)(2,1)}, u32[]{:S(2)}) copy-start(bf16[384,72]{0,1:T(8,128)(2,1)} %param.24) | copy-start | bytes 165892
  7.2 42.9 %copy-start.118 = (bf16[72,384]{1,0:T(8,128)(2,1)S(1)}, bf16[72,384]{1,0:T(8,128)(2,1)}, u32[]{:S(2)}) copy-start(bf16[72,384]{1,0:T(8,128)(2,1)} %param.23) | copy-start | bytes 165892
  7.2 42.9 %copy-start.119 = (bf16[72,384]{1,0:T(8,128)(2,1)S(1)}, bf16[72,384]{1,0:T(8,128)(2,1)}, u32[]{:S(2)}) copy-start(bf16[72,384]{1,0:T(8,128)(2,1)} %param.22) | copy-start | bytes 165892
  7.2 65.7 %all-gather.8.cloned.1.call-start = ((), (), s32[]{:S(2)}) async-start(), calls=%async_computation.5 | async-start | bytes 2949120 | tf_op jit(solution)/shard_map/all_gather | solution.py:167
  47.7 73.7 %all-gather.6.cloned.1.call-start = ((), (), s32[]{:S(2)}) async-start(), calls=%async_computation.4 | async-start | bytes 1492992 | tf_op jit(solution)/shard_map/all_gather | solution.py:166
  49.6 33.5 %copy-start.15 = (f32[1024,64]{0,1:T(8,128)}, f32[1024,64]{0,1:T(8,128)S(1)}, u32[]{:S(2)}) copy-start(f32[1024,64]{0,1:T(8,128)S(1)} %get-tuple-element.285) | copy-start | bytes 786436
  49.6 33.7 %copy-start.13 = (f32[1024,64]{0,1:T(8,128)}, f32[1024,64]{0,1:T(8,128)S(1)}, u32[]{:S(2)}) copy-start(f32[1024,64]{0,1:T(8,128)S(1)} %get-tuple-element.284) | copy-start | bytes 786436
  49.9 30.9 %copy-start.124 = (f32[1024]{0:T(1024)}, f32[1024]{0:T(1024)S(1)}, u32[]{:S(2)}) copy-start(f32[1024]{0:T(1024)S(1)} %add_rsqrt_fusion.1) | copy-start | bytes 12292
  50.1 83.7 %copy-start.35 = (pred[512,512]{0,1:T(8,128)(4,1)}, pred[512,512]{0,1:T(8,128)(4,1)S(1)}, u32[]{:S(2)}) copy-start(pred[512,512]{0,1:T(8,128)(4,1)S(1)} %fusion.121) | copy-start | bytes 786436
  51.4 34.6 %copy-start.19 = (pred[512,1024]{0,1:T(8,128)(4,1)}, pred[512,1024]{0,1:T(8,128)(4,1)S(1)}, u32[]{:S(2)}) copy-start(pred[512,1024]{0,1:T(8,128)(4,1)S(1)} %fusion.57) | copy-start | bytes 1572868
  74.9 5.9 %copy-start.120 = (f32[576]{0:T(1024)}, f32[576]{0:T(1024)S(1)}, u32[]{:S(2)}) copy-start(f32[576]{0:T(1024)S(1)} %get-tuple-element.173) | copy-start | bytes 6916
  77.4 52.1 %copy-start.72 = (bf16[576,48]{1,0:T(8,128)(2,1)}, bf16[576,48]{1,0:T(8,128)(2,1)S(1)}, u32[]{:S(2)}) copy-start(bf16[576,48]{1,0:T(8,128)(2,1)S(1)} %get-tuple-element.209) | copy-start | bytes 165892
  79.3 83.3 %all-gather.10.cloned.1.call-start = ((), (), s32[]{:S(2)}) async-start(), calls=%async_computation.6 | async-start | bytes 6635520 | tf_op jit(solution)/shard_map/all_gather | solution.py:167
  83.0 10.5 %copy-start.28 = (bf16[1024,192]{0,1:T(8,128)(2,1)}, bf16[1024,192]{0,1:T(8,128)(2,1)S(1)}, u32[]{:S(2)}) copy-start(bf16[1024,192]{0,1:T(8,128)(2,1)S(1)} %fusion.123) | copy-start | bytes 1179652
  84.1 9.4 %copy-start.52 = (bf16[512,192]{0,1:T(8,128)(2,1)}, bf16[512,192]{0,1:T(8,128)(2,1)S(1)}, u32[]{:S(2)}) copy-start(bf16[512,192]{0,1:T(8,128)(2,1)S(1)} %get-tuple-element.247) | copy-start | bytes 589828
  85.1 8.4 %copy-start = (f32[1024,512,3]{1,0,2:T(8,128)}, f32[1024,512,3]{1,0,2:T(8,128)S(1)}, u32[]{:S(2)}) copy-start(f32[1024,512,3]{1,0,2:T(8,128)S(1)} %fusion.139) | copy-start | bytes 18874372
  87.2 6.3 %copy-start.17 = (f32[1024,512,3]{1,0,2:T(8,128)}, f32[1024,512,3]{1,0,2:T(8,128)S(1)}, u32[]{:S(2)}) copy-start(f32[1024,512,3]{1,0,2:T(8,128)S(1)} %get-tuple-element.301) | copy-start | bytes 18874372
  87.3 6.3 %copy-start.157 = (f32[3,512]{1,0:T(4,128)}, f32[3,512]{1,0:T(4,128)S(1)}, u32[]{:S(2)}) copy-start(f32[3,512]{1,0:T(4,128)S(1)} %get-tuple-element.300) | copy-start | bytes 18436
  87.9 44.8 %copy-start.1 = (f32[512,512,3]{1,0,2:T(8,128)}, f32[512,512,3]{1,0,2:T(8,128)S(1)}, u32[]{:S(2)}) copy-start(f32[512,512,3]{1,0,2:T(8,128)S(1)} %fusion.145) | copy-start | bytes 9437188
  122.9 6.5 %copy-start.162 = (f32[3,512]{1,0:T(4,128)S(1)}, f32[3,512]{1,0:T(4,128)}, u32[]{:S(2)}) copy-start(f32[3,512]{1,0:T(4,128)} %get-tuple-element.177) | copy-start | bytes 18436
  122.9 6.5 %copy-start.147 = (f32[3,512]{1,0:T(4,128)S(1)}, f32[3,512]{1,0:T(4,128)}, u32[]{:S(2)}) copy-start(f32[3,512]{1,0:T(4,128)} %get-tuple-element.179) | copy-start | bytes 18436
  122.9 6.5 %copy-start.150 = (f32[3,512]{1,0:T(4,128)S(1)}, f32[3,512]{1,0:T(4,128)}, u32[]{:S(2)}) copy-start(f32[3,512]{1,0:T(4,128)} %get-tuple-element.178) | copy-start | bytes 18436
  123.0 6.5 %copy-start.158 = (f32[3,512]{1,0:T(4,128)S(1)}, f32[3,512]{1,0:T(4,128)}, u32[]{:S(2)}) copy-start(f32[3,512]{1,0:T(4,128)} %copy-done.157) | copy-start | bytes 18436
  123.0 6.5 %copy-start.8 = (bf16[1024,576]{0,1:T(8,128)(2,1)S(1)}, bf16[1024,576]{0,1:T(8,128)(2,1)}, u32[]{:S(2)}) copy-start(bf16[1024,576]{0,1:T(8,128)(2,1)} %param.13) | copy-start | bytes 3538948
  123.0 6.5 %copy-start.74 = (bf16[576,48]{1,0:T(8,128)(2,1)S(1)}, bf16[576,48]{1,0:T(8,128)(2,1)}, u32[]{:S(2)}) copy-start(bf16[576,48]{1,0:T(8,128)(2,1)} %get-tuple-element.214) | copy-start | bytes 165892
  123.0 6.5 %copy-start.76 = (bf16[576,48]{1,0:T(8,128)(2,1)S(1)}, bf16[576,48]{1,0:T(8,128)(2,1)}, u32[]{:S(2)}) copy-start(bf16[576,48]{1,0:T(8,128)(2,1)} %get-tuple-element.215) | copy-start | bytes 165892
  123.0 6.5 %copy-start.78 = (bf16[576,48]{1,0:T(8,128)(2,1)S(1)}, bf16[576,48]{1,0:T(8,128)(2,1)}, u32[]{:S(2)}) copy-start(bf16[576,48]{1,0:T(8,128)(2,1)} %get-tuple-element.216) | copy-start | bytes 165892
  123.0 6.5 %copy-start.121 = (f32[576]{0:T(1024)S(1)}, f32[576]{0:T(1024)}, u32[]{:S(2)}) copy-start(f32[576]{0:T(1024)} %copy-done.120) | copy-start | bytes 6916
  123.0 6.5 %copy-start.125 = (f32[1024]{0:T(1024)S(1)}, f32[1024]{0:T(1024)}, u32[]{:S(2)}) copy-start(f32[1024]{0:T(1024)} %copy-done.124) | copy-start | bytes 12292
  131.6 9.4 %copy-start.84 = (bf16[1024,192]{0,1:T(8,128)(2,1)}, bf16[1024,192]{0,1:T(8,128)(2,1)S(1)}, u32[]{:S(2)}) copy-start(bf16[1024,192]{0,1:T(8,128)(2,1)S(1)} %convolution_convert_fusion.6) | copy-start | bytes 1179652
  132.7 10.4 %copy-start.164 = (bf16[64,3,512]{2,0,1:T(8,128)(2,1)}, bf16[64,3,512]{2,0,1:T(8,128)(2,1)S(1)}, u32[]{:S(2)}) copy-start(bf16[64,3,512]{2,0,1:T(8,128)(2,1)S(1)} %fusion.71) | copy-start | bytes 589828
  134.7 8.4 %copy-start.166 = (bf16[64,3,512]{2,0,1:T(8,128)(2,1)}, bf16[64,3,512]{2,0,1:T(8,128)(2,1)S(1)}, u32[]{:S(2)}) copy-start(bf16[64,3,512]{2,0,1:T(8,128)(2,1)S(1)} %fusion.70) | copy-start | bytes 589828
  136.9 6.3 %copy-start.168 = (bf16[64,3,512]{2,0,1:T(8,128)(2,1)}, bf16[64,3,512]{2,0,1:T(8,128)(2,1)S(1)}, u32[]{:S(2)}) copy-start(bf16[64,3,512]{2,0,1:T(8,128)(2,1)S(1)} %fusion.72) | copy-start | bytes 589828
  144.4 56.9 %copy-start.10 = (f32[1024,576]{0,1:T(8,128)}, f32[1024,576]{0,1:T(8,128)S(1)}, u32[]{:S(2)}) copy-start(f32[1024,576]{0,1:T(8,128)S(1)} %get-tuple-element.307) | copy-start | bytes 7077892
  145.1 112.8 %copy-start.127 = (f32[3,512]{1,0:T(4,128)}, f32[3,512]{1,0:T(4,128)S(1)}, u32[]{:S(2)}) copy-start(f32[3,512]{1,0:T(4,128)S(1)} %get-tuple-element.291) | copy-start | bytes 18436
  145.1 112.8 %copy-start.129 = (f32[3,512]{1,0:T(4,128)}, f32[3,512]{1,0:T(4,128)S(1)}, u32[]{:S(2)}) copy-start(f32[3,512]{1,0:T(4,128)S(1)} %get-tuple-element.319) | copy-start | bytes 18436
  165.8 7.9 %copy-start.80 = (bf16[576,384]{1,0:T(8,128)(2,1)}, bf16[576,384]{1,0:T(8,128)(2,1)S(1)}, u32[]{:S(2)}) copy-start(bf16[576,384]{1,0:T(8,128)(2,1)S(1)} %get-tuple-element.195) | copy-start | bytes 1327108
  165.8 7.9 %copy-start.81 = (bf16[576,384]{1,0:T(8,128)(2,1)}, bf16[576,384]{1,0:T(8,128)(2,1)S(1)}, u32[]{:S(2)}) copy-start(bf16[576,384]{1,0:T(8,128)(2,1)S(1)} %get-tuple-element.196) | copy-start | bytes 1327108
  165.8 7.9 %copy-start.82 = (bf16[576,384]{1,0:T(8,128)(2,1)}, bf16[576,384]{1,0:T(8,128)(2,1)S(1)}, u32[]{:S(2)}) copy-start(bf16[576,384]{1,0:T(8,128)(2,1)S(1)} %get-tuple-element.197) | copy-start | bytes 1327108
  165.9 7.9 %copy-start.83 = (bf16[576,384]{1,0:T(8,128)(2,1)}, bf16[576,384]{1,0:T(8,128)(2,1)S(1)}, u32[]{:S(2)}) copy-start(bf16[576,384]{1,0:T(8,128)(2,1)S(1)} %get-tuple-element.198) | copy-start | bytes 1327108
  183.3 7.1 %copy-start.176 = (bf16[1024,1536]{1,0:T(8,128)(2,1)}, bf16[1024,1536]{1,0:T(8,128)(2,1)S(1)}, u32[]{:S(2)}) copy-start(bf16[1024,1536]{1,0:T(8,128)(2,1)S(1)} %get-tuple-element.192) | copy-start | bytes 9437188
  183.3 5.1 %copy-start.178 = (bf16[1024,1536]{1,0:T(8,128)(2,1)S(1)}, bf16[1024,1536]{1,0:T(8,128)(2,1)}, u32[]{:S(2)}) copy-start(bf16[1024,1536]{1,0:T(8,128)(2,1)} %get-tuple-element.193) | copy-start | bytes 9437188
  206.1 9.6 %slice-start.2 = ((s8[6291456]{0:T(1024)(128)(4,1)}), s8[4194304]{0:T(1024)(128)(4,1)S(1)}, s32[]{:S(2)}) async-start(s8[6291456]{0:T(1024)(128)(4,1)} %bitcast.585), calls=%async_computation.9 | async-start | bytes 8388608
  208.4 42.1 %copy-start.58 = (bf16[512,192]{0,1:T(8,128)(2,1)}, bf16[512,192]{0,1:T(8,128)(2,1)S(1)}, u32[]{:S(2)}) copy-start(bf16[512,192]{0,1:T(8,128)(2,1)S(1)} %get-tuple-element.239) | copy-start | bytes 589828
  208.4 42.8 %copy-start.60 = (bf16[512,192]{0,1:T(8,128)(2,1)}, bf16[512,192]{0,1:T(8,128)(2,1)S(1)}, u32[]{:S(2)}) copy-start(bf16[512,192]{0,1:T(8,128)(2,1)S(1)} %get-tuple-element.243) | copy-start | bytes 589828
  208.4 7.3 %slice-start.3 = ((s8[6291456]{0:T(1024)(128)(4,1)}), s8[2097152]{0:T(1024)(128)(4,1)S(1)}, s32[]{:S(2)}) async-start(s8[6291456]{0:T(1024)(128)(4,1)} %bitcast.585), calls=%async_computation.10 | async-start | bytes 4194304
  212.1 6.4 %slice-start.6 = ((s8[6291456]{0:T(1024)(128)(4,1)}), s8[4194304]{0:T(1024)(128)(4,1)S(1)}, s32[]{:S(2)}) async-start(s8[6291456]{0:T(1024)(128)(4,1)} %bitcast.589), calls=%async_computation.13 | async-start | bytes 8388608
  215.8 5.6 %slice-start.10 = ((s8[6291456]{0:T(1024)(128)(4,1)}), s8[4194304]{0:T(1024)(128)(4,1)S(1)}, s32[]{:S(2)}) async-start(s8[6291456]{0:T(1024)(128)(4,1)} %bitcast.595), calls=%async_computation.17 | async-start | bytes 8388608
  235.3 12.7 %copy-start.57 = (bf16[512,192]{0,1:T(8,128)(2,1)S(1)}, bf16[512,192]{0,1:T(8,128)(2,1)}, u32[]{:S(2)}) copy-start(bf16[512,192]{0,1:T(8,128)(2,1)} %copy-done.56) | copy-start | bytes 589828
  257.9 5.6 %copy-start.55 = (bf16[512,192]{0,1:T(8,128)(2,1)S(1)}, bf16[512,192]{0,1:T(8,128)(2,1)}, u32[]{:S(2)}) copy-start(bf16[512,192]{0,1:T(8,128)(2,1)} %copy-done.54) | copy-start | bytes 589828
  276.0 6.8 %copy-start.16 = (f32[1024,64]{0,1:T(8,128)S(1)}, f32[1024,64]{0,1:T(8,128)}, u32[]{:S(2)}) copy-start(f32[1024,64]{0,1:T(8,128)} %copy-done.15) | copy-start | bytes 786436
  276.0 65.5 %all-to-all-start = ((bf16[4,576,1152]{2,1,0:T(8,128)(2,1)}), bf16[4,576,1152]{2,1,0:T(8,128)(2,1)}, u32[]{:S(2)}, u32[]{:S(2)}) async-start(bf16[4,576,1152]{2,1,0:T(8,128)(2,1)} %maximum_maximum_fusion), calls=%async_computation | async-start | bytes 10616832 | tf_op jit(solution)/shard_map/all_to_all | solution.py:201
  284.7 7.4 %copy-start.101 = (bf16[512,64]{0,1:T(8,128)(2,1)}, bf16[512,64]{0,1:T(8,128)(2,1)S(1)}, u32[]{:S(2)}) copy-start(bf16[512,64]{0,1:T(8,128)(2,1)S(1)} %slice.903) | copy-start | bytes 196612
  284.8 7.4 %copy-start.103 = (bf16[512,64]{0,1:T(8,128)(2,1)}, bf16[512,64]{0,1:T(8,128)(2,1)S(1)}, u32[]{:S(2)}) copy-start(bf16[512,64]{0,1:T(8,128)(2,1)S(1)} %slice.904) | copy-start | bytes 196612
  285.1 7.1 %copy-start.105 = (bf16[512,64]{0,1:T(8,128)(2,1)}, bf16[512,64]{0,1:T(8,128)(2,1)S(1)}, u32[]{:S(2)}) copy-start(bf16[512,64]{0,1:T(8,128)(2,1)S(1)} %slice.905) | copy-start | bytes 196612
  349.0 7.5 %copy-start.63 = (bf16[576,144]{0,1:T(8,128)(2,1)S(1)}, bf16[576,144]{0,1:T(8,128)(2,1)}, u32[]{:S(2)}) copy-start(bf16[576,144]{0,1:T(8,128)(2,1)} %get-tuple-element.257) | copy-start | bytes 497668
  349.0 7.5 %copy-start.107 = (bf16[576,48]{0,1:T(8,128)(2,1)S(1)}, bf16[576,48]{0,1:T(8,128)(2,1)}, u32[]{:S(2)}) copy-start(bf16[576,48]{0,1:T(8,128)(2,1)} %get-tuple-element.274) | copy-start | bytes 165892
  349.0 7.5 %copy-start.108 = (bf16[576,48]{0,1:T(8,128)(2,1)S(1)}, bf16[576,48]{0,1:T(8,128)(2,1)}, u32[]{:S(2)}) copy-start(bf16[576,48]{0,1:T(8,128)(2,1)} %get-tuple-element.278) | copy-start | bytes 165892
  349.0 12.8 %copy-start.62 = (bf16[576,144]{0,1:T(8,128)(2,1)S(1)}, bf16[576,144]{0,1:T(8,128)(2,1)}, u32[]{:S(2)}) copy-start(bf16[576,144]{0,1:T(8,128)(2,1)} %get-tuple-element.256) | copy-start | bytes 497668
  375.3 32.1 %all-to-all-start.1 = ((bf16[4,576,512]{2,1,0:T(8,128)(2,1)}), bf16[4,576,512]{2,1,0:T(8,128)(2,1)S(1)}, u32[]{:S(2)}, u32[]{:S(2)}) async-start(bf16[4,576,512]{2,1,0:T(8,128)(2,1)} %copy.350), calls=%async_computation.1 | async-start | bytes 4718592 | tf_op jit(solution)/shard_map/all_to_all | solution.py:201
  407.3 37.1 %all-to-all-start.3 = ((bf16[8,72,1152]{2,1,0:T(8,128)(2,1)}), bf16[8,72,1152]{2,1,0:T(8,128)(2,1)}, u32[]{:S(2)}, u32[]{:S(2)}) async-start(bf16[8,72,1152]{2,1,0:T(8,128)(2,1)} %bitcast.601), calls=%async_computation.3 | async-start | bytes 2654208 | tf_op jit(solution)/shard_map/all_to_all | solution.py:207
  444.4 19.7 %all-to-all-start.2 = ((bf16[8,72,512]{2,1,0:T(8,128)(2,1)}), bf16[8,72,512]{2,1,0:T(8,128)(2,1)S(1)}, u32[]{:S(2)}, u32[]{:S(2)}) async-start(bf16[8,72,512]{2,1,0:T(8,128)(2,1)} %bitcast.616), calls=%async_computation.2 | async-start | bytes 1179648 | tf_op jit(solution)/shard_map/all_to_all | solution.py:207
  (134 other events, 302.3 us)
Sparse Core Ops, SparseCore 0:
  47.8 25.0 all-gather.7
  79.4 41.9 all-gather.5
  123.0 39.6 all-gather.9
